TPU v7x, 256 devices: a whole 4x4x8 slice. The times are simulated.
256 devices in a mesh: seq: 32 (over x, z), tensor: 8 (over y, core).
Axes of the slice: x: 4, y: 4, z: 8, core: 2. Of those that a mesh axis runs over, the one named last changes fastest.
Arguments:
- hidden_in: bfloat16 [8192, 4096], P(('seq', 'tensor')), may hold values from -30 to 30
- prev_amax: float32 [], replicated, may hold values from 5 to 9
- w_x: bfloat16 [4096, 8192], P('seq', 'tensor'), may hold values from -0.09375 to 0.09375
- w_bc: bfloat16 [4096, 8, 2, 128], P('seq', 'tensor'), may hold values from -0.046875 to 0.046875
- w_dt: bfloat16 [4096, 128], P('seq', 'tensor'), may hold values from -0.09375 to 0.09375
- conv_x: float32 [4, 8192], P(None, 'tensor'), may hold values from -4 to 4
- conv_bc: float32 [4, 8, 2, 128], P(None, 'tensor'), may hold values from -4 to 4
- conv_state_x: bfloat16 [3, 8192], P(None, 'tensor'), may hold values from -6 to 6
- conv_state_bc: bfloat16 [3, 8, 2, 128], P(None, 'tensor'), may hold values from -3 to 3
- dt_bias: float32 [128], P('tensor'), may hold values from -2 to 1
- decay_rate: float32 [128], P('tensor'), may hold values from 1.2207031e-05 to 0.12
- skip: float32 [128], P('tensor'), may hold values from 0.5 to 4
- init_state: float32 [128, 64, 128], P('tensor'), may hold values from -48 to 48
- norm_gain: float32 [8192], P('tensor'), may hold values from 0.1 to 1.9
- w_out: bfloat16 [8192, 4096], P('tensor', 'seq'), may hold values from -0.0625 to 0.0625
Outputs:
- layer_out: bfloat16 [8192, 4096], P(('seq', 'tensor'))
- abs_max: float32 [], replicated
All inputs are finite; a program needn't handle non-finite values.
Results may differ from a plain program's by a relative error of at most 0.019.
Values may be sent and summed in bfloat16 or wider, within the bound.
A program may use at most 64 MiB of HBM per device.

v0:
```python
import jax
import jax.numpy as jnp
from jax import lax
from jax.sharding import Mesh
from jax.sharding import PartitionSpec as P

HEADS = 128
HEAD_DIM = 64
STATE = 128
GROUPS = 8
KERNEL = 4
SPAN = 128
SEQ = ("seq_0", "seq_1")
SEQ_TENSOR = ("seq_0", "seq_1", "tensor")


epsilon = 1e-05
quant_range = 448.0


def in_order(parts, dim):
    dims = list(parts.shape[1:])
    dims[dim] *= parts.shape[0]
    return jnp.moveaxis(parts, 0, dim).reshape(dims)


def sent_to_all(shard, axis):
    count = lax.axis_size(axis)
    return lax.all_to_all(
        jnp.broadcast_to(shard[None], (count, *shard.shape)), axis, 0, 0, tiled=True
    )


def gather_directly(shard, axis, dim):
    return in_order(sent_to_all(shard, axis), dim)


def over_copies(shard, axis):
    everything = sent_to_all(shard, axis)
    return jnp.max(everything, axis=0)


def sent_together(arrays, axis, dim, along):
    ends, at = ([], 0)
    for a in arrays[:-1]:
        at += a.shape[along]
        ends.append(at)
    both = jnp.concatenate(arrays, axis=along)
    return tuple(jnp.split(lax.all_gather(both, axis, axis=dim, tiled=True), ends, axis=along))


def from_behind(value, axis, steps):
    count = lax.axis_size(axis)
    first, last = (max(0, -steps), min(count, count - steps))
    return lax.ppermute(value, axis, [(source, source + steps) for source in range(first, last)])


def neutral_like(shard, identity):
    return jax.tree.map(
        lambda a, e: jnp.broadcast_to(jnp.asarray(e, a.dtype), a.shape), shard, identity
    )


def prefix_by_axis(shard, axes, combine, identity):
    before = start = neutral_like(shard, identity)
    total = shard
    for axis in reversed(axes):
        count, here = (lax.axis_size(axis), lax.axis_index(axis))
        pieces = jax.tree.map(
            lambda part, kind: lax.all_gather(part.astype(kind), axis),
            total,
            (jnp.bfloat16, jnp.bfloat16),
        )
        inside, total = (start, start)
        for k in range(count):
            passed = k < here
            total = combine(
                total, jax.tree.map(lambda part, own: part[k].astype(own.dtype), pieces, shard)
            )
            inside = jax.tree.map(lambda new, old: jnp.where(passed, new, old), total, inside)
        before = combine(inside, before)
    return before


def taken_together(shard, axis):
    return sent_to_all(shard, axis).sum(axis=0)


def cut_along(shard, dim, count):
    before, after = (shard.shape[:dim], shard.shape[dim + 1 :])
    return jnp.moveaxis(shard.reshape(*before, count, -1, *after), dim, 0)


def sent_and_summed(shard, axis, dim):
    parts = cut_along(shard, dim, lax.axis_size(axis))
    arrived = lax.all_to_all(parts, axis, split_axis=0, concat_axis=0, tiled=True)
    return arrived.astype(jnp.float32).sum(axis=0)


def depthwise(before, projected, conv_taps, length):
    extended = jnp.concatenate([before, projected], axis=0)
    summed = conv_taps[0] * extended[0:length]
    for offset in range(1, KERNEL):
        summed = summed + conv_taps[offset] * extended[offset : offset + length]
    return jax.nn.silu(summed).astype(jnp.bfloat16)


def combine(earlier, later):
    return (earlier[0] * later[0], later[0][:, None, None] * earlier[1] + later[1])


def local(
    hidden_in,
    prev_amax,
    w_x,
    w_bc,
    w_dt,
    conv_x,
    conv_bc,
    conv_state_x,
    conv_state_bc,
    dt_bias,
    decay_rate,
    skip,
    init_state,
    norm_gain,
    w_out,
):
    margin = KERNEL - 1
    gathered = gather_directly(hidden_in, "tensor", 0)
    abs_max = over_copies(jnp.max(jnp.abs(gathered.astype(jnp.float32))), SEQ)
    in_scale = prev_amax / quant_range
    leading = lax.axis_index(SEQ) == 0
    row_count = gathered.shape[0]
    bc_width = w_bc.shape[1] * w_bc.shape[2] * w_bc.shape[3]
    bc_rows = jnp.reshape(w_bc, (w_bc.shape[0], bc_width))
    scaled = gathered.astype(jnp.float32) * (quant_range / prev_amax)
    quant = jnp.clip(scaled, -quant_range, quant_range).astype(jnp.bfloat16)
    pieces = sent_together((w_x, bc_rows, w_dt), SEQ, 0, 1)
    x_proj, bc_proj, dt_proj = tuple(
        (
            jnp.dot(quant, weight_piece, preferred_element_type=jnp.float32)
            for weight_piece in pieces
        )
    )
    x_whole = (x_proj * in_scale).astype(jnp.bfloat16)
    bc_whole = (bc_proj * in_scale).astype(jnp.bfloat16)
    dt_raw = dt_proj * in_scale
    state_bc = jnp.reshape(conv_state_bc, (margin, bc_width))
    received = from_behind((x_whole[row_count - margin :], bc_whole[row_count - margin :]), SEQ, 1)
    x_edge = jnp.where(leading, conv_state_x, received[0])
    bc_edge = jnp.where(leading, state_bc, received[1])
    x_act = depthwise(x_edge, x_whole, conv_x, row_count)
    bc_act = depthwise(bc_edge, bc_whole, jnp.reshape(conv_bc, (KERNEL, bc_width)), row_count)
    step_size = jax.nn.softplus(dt_raw + dt_bias)
    heads_here = step_size.shape[1]
    groups_here = w_bc.shape[1]
    per_group = HEADS // GROUPS
    blocks = row_count // SPAN
    x_blocks = x_act.reshape(blocks, SPAN, heads_here, HEAD_DIM)
    bc_blocks = bc_act.reshape(blocks, SPAN, groups_here, 2, STATE)
    in_map = bc_blocks[:, :, :, 0]
    out_map = bc_blocks[:, :, :, 1]
    step_blocks = step_size.reshape(blocks, SPAN, heads_here)
    cum_blocks = jnp.cumsum(-step_blocks * decay_rate, axis=1)
    index_row = jnp.arange(SPAN, dtype=jnp.int32)
    lower_mask = index_row[:, None] >= index_row[None, :]
    intersection = jnp.einsum(
        "ctgn,cugn->cgtu", out_map, in_map, preferred_element_type=jnp.float32
    )
    intersection = jnp.repeat(intersection, per_group, axis=1)
    cum_heads = jnp.transpose(cum_blocks, (0, 2, 1))
    log_gap = cum_heads[:, :, :, None] - cum_heads[:, :, None, :]
    decay = jnp.exp(jnp.where(lower_mask[None, None], log_gap, -1e30))
    step_heads = jnp.transpose(step_blocks, (0, 2, 1))
    weights = (intersection * decay * step_heads[:, :, None, :]).astype(jnp.bfloat16)
    local_part = jnp.einsum(
        "chtu,cuhp->cthp", weights, x_blocks, preferred_element_type=jnp.float32
    )
    last_cum = cum_blocks[:, SPAN - 1, :]
    x_weighted = (
        x_blocks.astype(jnp.float32)
        * (step_blocks * jnp.exp(last_cum[:, None, :] - cum_blocks))[:, :, :, None]
    ).astype(jnp.bfloat16)
    in_heads = jnp.repeat(in_map, per_group, axis=2)
    added = jnp.einsum("cuhp,cuhn->chpn", x_weighted, in_heads, preferred_element_type=jnp.float32)

    def carry_on(carried, element):
        block_decay, block_added = element
        return (block_decay[:, None, None] * carried + block_added, carried)

    empty_state = jnp.zeros((heads_here, HEAD_DIM, STATE), jnp.float32)
    device_state, entering = lax.scan(carry_on, empty_state, (jnp.exp(last_cum), added))
    device_decay = jnp.exp(jnp.sum(last_cum, axis=0))
    seeded = device_state + jnp.where(leading, device_decay[:, None, None] * init_state, 0.0)
    identity = (jnp.ones_like(device_decay), jnp.zeros_like(device_state))
    scanned = prefix_by_axis((device_decay, seeded), SEQ, combine, identity)
    incoming = jnp.where(leading, init_state, scanned[1])
    prefix = jnp.exp(jnp.cumsum(last_cum, axis=0) - last_cum)
    states_in = entering + prefix[:, :, None, None] * incoming[None]
    out_heads = jnp.repeat(out_map, per_group, axis=2).astype(jnp.float32)
    carried_part = (
        jnp.einsum("cthn,chpn->cthp", out_heads, states_in, precision=lax.Precision.HIGHEST)
        * jnp.exp(cum_blocks)[:, :, :, None]
    )
    ssm_out = local_part + carried_part + skip[None, None, :, None] * x_blocks.astype(jnp.float32)
    ssm_out = ssm_out.reshape(row_count, heads_here * HEAD_DIM)
    squares = taken_together(jnp.sum(ssm_out * ssm_out, axis=1), "tensor")
    mean_sq = squares / (HEADS * HEAD_DIM)
    normed = (ssm_out * lax.rsqrt(mean_sq + epsilon)[:, None] * norm_gain).astype(jnp.bfloat16)
    partial_out = jnp.dot(
        normed, lax.all_gather(w_out, SEQ, axis=1, tiled=True), preferred_element_type=jnp.float32
    )
    layer_out = sent_and_summed(partial_out.astype(jnp.bfloat16), "tensor", 0).astype(jnp.bfloat16)
    return (layer_out, abs_max)


def solution(mesh):
    finer = Mesh(mesh.devices.reshape(4, 8, mesh.shape["tensor"]), ("seq_0", "seq_1", "tensor"))
    return jax.shard_map(
        local,
        mesh=finer,
        in_specs=(
            P(SEQ_TENSOR, None),
            P(),
            P(SEQ, "tensor"),
            P(SEQ, "tensor", None, None),
            P(SEQ, "tensor"),
            P(None, "tensor"),
            P(None, "tensor", None, None),
            P(None, "tensor"),
            P(None, "tensor", None, None),
            P("tensor"),
            P("tensor"),
            P("tensor"),
            P("tensor", None, None),
            P("tensor"),
            P("tensor", SEQ),
        ),
        out_specs=(P(SEQ_TENSOR, None), P()),
        check_vma=False,
    )
```

profile of v0, /device:TPU:2, one launch (start us, length us, event | category | flops | bytes accessed | tf_op | source)
XLA Modules:
  0.0 372.0 jit_solution(1133156709951974368)
XLA Ops:
  8.9 1.7 pad_maximum_fusion.1
  10.6 2.6 broadcast_in_dim.26
  13.2 4.6 %all-to-all-start = ((bf16[8,32,4096]{2,1,0:T(8,128)(2,1)}), bf16[8,32,4096]{2,1,0:T(8,128)(2,1)S(1)}, u32[]{:S(2)}, u32[]{:S(2)}) async-start(bf16[8,32,4096]{2,1,0:T(8,128)(2,1)} %broadcast_in_dim.26), calls=%async_computation | async-start | bytes 4194304 | tf_op jit(solution)/shard_map/all_to_all | solution.py:29
  18.7 26.3 %all-to-all-done = bf16[8,32,4096]{2,1,0:T(8,128)(2,1)S(1)} async-done(((bf16[8,32,4096]{2,1,0:T(8,128)(2,1)}), bf16[8,32,4096]{2,1,0:T(8,128)(2,1)S(1)}, u32[]{:S(2)}, u32[]{:S(2)}) %all-to-all-start) | async-done | bytes 2097184 | tf_op jit(solution)/shard_map/all_to_all | solution.py:29
  45.0 2.6 fusion.5
  47.6 78.4 %all-gather.8.cloned.1.call-done = bf16[4096,1296]{1,0:T(8,128)(2,1)} async-done(((bf16[128,1296]{1,0:T(8,128)(2,1)}), bf16[4096,1296]{1,0:T(8,128)(2,1)}) %all-gather.8.cloned.1.call-update) | async-done | bytes 10616848 | tf_op jit(solution)/shard_map/all_gather | solution.py:49
  126.0 2.7 compare_select_fusion
  129.7 2.3 fusion.20
  132.7 2.0 collective-permute-start.1
  134.8 5.7 %fusion.14 = bf16[256,1024]{1,0:T(8,128)(2,1)S(1)} fusion(bf16[256,4096]{1,0:T(8,128)(2,1)S(1)} %bitcast.201, bf16[4096,1296]{1,0:T(8,128)(2,1)} %all-gather.8.cloned.1.call-done, f32[]{:T(128)S(6)} %div.21), kind=kOutput, calls=%fused_computation.23 | convolution fusion | flops 2148007936 | bytes 11010052 | tf_op jit(solution)/shard_map/dot_general | solution.py:142
  140.5 3.2 collective-permute-start
  144.4 1.0 copy.80
  145.4 1.3 multiply_convert_fusion.3
  150.8 2.0 while.13
  155.2 16.5 %all-reduce = bf16[128]{0:T(256)(128)(2,1)S(1)} all-reduce(bf16[128]{0:T(256)(128)(2,1)S(1)} %dynamic-update-slice), channel_id=2, replica_groups=mesh['seq_0'=4,'seq_1'=8,'tensor'=8] {'seq_1'}, use_global_device_ids=true, to_apply=%add | all-reduce | flops 128 | bytes 512
  172.4 20.9 %all-gather.14.cloned.1.call-done = bf16[128,64,128]{2,1,0:T(8,128)(2,1)} async-done(((bf16[16,64,128]{2,1,0:T(8,128)(2,1)}), bf16[128,64,128]{2,1,0:T(8,128)(2,1)}) %all-gather.14.cloned.1.call-update) | async-done | bytes 2097168 | tf_op jit(solution)/shard_map/all_gather | solution.py:70
  193.3 2.8 fusion.80
  196.8 8.2 %all-gather.2 = bf16[4,1,16]{2,1,0:T(2,128)(2,1)S(1)} all-gather(bf16[1,1,16]{2,1,0:T(2,128)(2,1)S(1)} %fusion.91), channel_id=1, replica_groups=mesh['seq_0'=4,'seq_1'=8,'tensor'=8] {'seq_0'}, dimensions={0}, use_global_device_ids=true | all-gather | bytes 160 | tf_op jit(solution)/shard_map/all_gather | solution.py:70
  205.1 1.1 copy.102
  206.4 1.9 convolution_bitcast_fusion.1
  208.3 12.3 %all-gather.10.cloned.1.call-done = bf16[4,16,64,128]{3,2,1,0:T(8,128)(2,1)} async-done(((bf16[1,16,64,128]{3,2,1,0:T(8,128)(2,1)}), bf16[4,16,64,128]{3,2,1,0:T(8,128)(2,1)}) %all-gather.10.cloned.1.call-update) | async-done | bytes 1048592 | tf_op jit(solution)/shard_map/all_gather | solution.py:70
  220.6 3.1 fusion.46
  223.8 2.2 multiply_reduce_fusion
  226.6 4.3 %all-to-all-start.1 = ((f32[8,1,256]{2,1,0:T(1,128)}), f32[8,1,256]{2,1,0:T(1,128)S(1)}, u32[]{:S(2)}, u32[]{:S(2)}) async-start(f32[8,1,256]{2,1,0:T(1,128)} %broadcast_in_dim.33), calls=%async_computation.1 | async-start | bytes 16384 | tf_op jit(solution)/shard_map/all_to_all | solution.py:29
  231.7 4.5 %all-to-all-done.1 = f32[8,1,256]{2,1,0:T(1,128)S(1)} async-done(((f32[8,1,256]{2,1,0:T(1,128)}), f32[8,1,256]{2,1,0:T(1,128)S(1)}, u32[]{:S(2)}, u32[]{:S(2)}) %all-to-all-start.1) | async-done | bytes 8224 | tf_op jit(solution)/shard_map/all_to_all | solution.py:29
  236.2 1.3 broadcast_in_dim.35
  237.4 10.4 %all-to-all-start.3 = ((f32[32,1,1]{2,1,0:T(1,128)}), f32[32,1,1]{2,1,0:T(1,128)S(1)}, u32[]{:S(2)}, u32[]{:S(2)}) async-start(f32[32,1,1]{2,1,0:T(1,128)} %broadcast_in_dim.35), calls=%async_computation.3 | async-start | bytes 32768 | tf_op jit(solution)/shard_map/all_to_all | solution.py:29
  247.9 77.9 %all-gather.12.cloned.1.call-done = bf16[1024,4096]{1,0:T(8,128)(2,1)} async-done(((bf16[1024,128]{1,0:T(8,128)(2,1)}), bf16[1024,4096]{1,0:T(8,128)(2,1)}) %all-gather.12.cloned.1.call-update) | async-done | bytes 8388624 | tf_op jit(solution)/shard_map/all_gather | solution.py:212
  325.7 7.2 %convolution_convert_fusion = bf16[256,4096]{1,0:T(8,128)(2,1)} fusion(bf16[1024,4096]{1,0:T(8,128)(2,1)} %all-gather.12.cloned.1.call-done, f32[128,8,2,128]{3,2,1,0:T(2,128)S(1)} %bitcast.202, f32[1024]{0:T(1024)S(1)} %copy-done.6, f32[256]{0:T(256)S(1)} %add_rsqrt_fusion), kind=kOutput, calls=%fused_computation.8 | convolution fusion | flops 2149318656 | bytes 11539456 | tf_op jit(solution)/shard_map/dot_general | solution.py:211
  333.0 4.3 %all-to-all-start.2 = ((bf16[8,32,4096]{2,1,0:T(8,128)(2,1)}), bf16[8,32,4096]{2,1,0:T(8,128)(2,1)S(1)}, u32[]{:S(2)}, u32[]{:S(2)}) async-start(bf16[8,32,4096]{2,1,0:T(8,128)(2,1)} %bitcast.37), calls=%async_computation.2 | async-start | bytes 4194304 | tf_op jit(solution)/shard_map/all_to_all | solution.py:96
  337.9 26.5 %all-to-all-done.2 = bf16[8,32,4096]{2,1,0:T(8,128)(2,1)S(1)} async-done(((bf16[8,32,4096]{2,1,0:T(8,128)(2,1)}), bf16[8,32,4096]{2,1,0:T(8,128)(2,1)S(1)}, u32[]{:S(2)}, u32[]{:S(2)}) %all-to-all-start.2) | async-done | bytes 2097184 | tf_op jit(solution)/shard_map/all_to_all | solution.py:96
  364.4 1.1 reduce_sum.42
  (100 shorter events, 15.7 us)
Async XLA Ops:
  7.2 118.8 %all-gather.8.cloned.1.call-start = ((), (), s32[]{:S(2)}) async-start(), calls=%async_computation.4 | async-start | bytes 11894784 | tf_op jit(solution)/shard_map/all_gather | solution.py:49
  13.2 5.4 %copy-start.11 = (f32[4,1,2,128]{3,2,1,0:T(2,128)S(1)}, f32[4,1,2,128]{3,2,1,0:T(2,128)}, u32[]{:S(2)}) copy-start(f32[4,1,2,128]{3,2,1,0:T(2,128)} %param.23) | copy-start | bytes 12292
  13.2 5.4 %copy-start.7 = (f32[4,1024]{1,0:T(4,128)S(1)}, f32[4,1024]{1,0:T(4,128)}, u32[]{:S(2)}) copy-start(f32[4,1024]{1,0:T(4,128)} %param.22) | copy-start | bytes 49156
  13.2 31.8 %all-to-all-start = ((bf16[8,32,4096]{2,1,0:T(8,128)(2,1)}), bf16[8,32,4096]{2,1,0:T(8,128)(2,1)S(1)}, u32[]{:S(2)}, u32[]{:S(2)}) async-start(bf16[8,32,4096]{2,1,0:T(8,128)(2,1)} %broadcast_in_dim.26), calls=%async_computation | async-start | bytes 4194304 | tf_op jit(solution)/shard_map/all_to_all | solution.py:29
  17.9 175.5 %all-gather.14.cloned.1.call-start = ((), (), s32[]{:S(2)}) async-start(), calls=%async_computation.7 | async-start | bytes 2359296 | tf_op jit(solution)/shard_map/all_gather | solution.py:70
  18.7 107.3 %copy-start.15 = (f32[16]{0:T(128)S(1)}, f32[16]{0:T(128)}, u32[]{:S(2)}) copy-start(f32[16]{0:T(128)} %param.26) | copy-start | bytes 196
  47.6 81.2 %copy-start.16 = (f32[16]{0:T(128)S(1)}, f32[16]{0:T(128)}, u32[]{:S(2)}) copy-start(f32[16]{0:T(128)} %param.27) | copy-start | bytes 196
  126.0 3.8 %copy-start = (bf16[8,32,4096]{2,1,0:T(8,128)(2,1)S(1)}, bf16[8,32,4096]{2,1,0:T(8,128)(2,1)}, u32[]{:S(2)}) copy-start(bf16[8,32,4096]{2,1,0:T(8,128)(2,1)} %get-tuple-element.61) | copy-start | bytes 6291460
  132.1 0.7 copy-start.5
  132.7 12.6 %copy-start.14 = (bf16[3,1,2,128]{3,2,1,0:T(2,128)(2,1)S(1)}, bf16[3,1,2,128]{3,2,1,0:T(2,128)(2,1)}, u32[]{:S(2)}) copy-start(bf16[3,1,2,128]{3,2,1,0:T(2,128)(2,1)} %param.25) | copy-start | bytes 4612
  132.7 15.4 %copy-start.8 = (bf16[3,1024]{1,0:T(4,128)(2,1)S(1)}, bf16[3,1024]{1,0:T(4,128)(2,1)}, u32[]{:S(2)}) copy-start(bf16[3,1024]{1,0:T(4,128)(2,1)} %param.24) | copy-start | bytes 18436
  132.7 12.6 %collective-permute-start.1 = (bf16[3,256]{1,0:T(4,128)(2,1)S(1)}, bf16[3,256]{1,0:T(4,128)(2,1)S(1)}, u32[]{:S(2)}, u32[]{:S(2)}) collective-permute-start(bf16[3,256]{1,0:T(4,128)(2,1)S(1)} %slice.201), channel_id=1, source_target_pairs={{0,8},{8,16},{16,24},{24,32},{32,40},{40,48},{48,56},{56,64},{64,7... | collective-permute-start | bytes 4616 | tf_op jit(solution)/shard_map/ppermute | solution.py:55
  140.5 7.7 %collective-permute-start = (bf16[3,1024]{1,0:T(4,128)(2,1)S(1)}, bf16[3,1024]{1,0:T(4,128)(2,1)S(1)}, u32[]{:S(2)}, u32[]{:S(2)}) collective-permute-start(bf16[3,1024]{1,0:T(4,128)(2,1)S(1)} %slice.196), channel_id=1, source_target_pairs={{0,8},{8,16},{16,24},{24,32},{32,40},{40,48},{48,56},{56,64},{64,7... | collective-permute-start | bytes 18440 | tf_op jit(solution)/shard_map/ppermute | solution.py:55
  150.8 2.0 copy-start.2
  150.8 3.0 copy-start.18
  153.7 66.9 %all-gather.10.cloned.1.call-start = ((), (), s32[]{:S(2)}) async-start(), calls=%async_computation.5 | async-start | bytes 1310720 | tf_op jit(solution)/shard_map/all_gather | solution.py:70
  172.3 32.6 %copy-start.9 = (f32[16]{0:T(128)}, f32[16]{0:T(128)S(1)}, u32[]{:S(2)}) copy-start(f32[16]{0:T(128)S(1)} %get-tuple-element.82) | copy-start | bytes 196
  196.1 129.6 %all-gather.12.cloned.1.call-start = ((), (), s32[]{:S(2)}) async-start(), calls=%async_computation.6 | async-start | bytes 8650752 | tf_op jit(solution)/shard_map/all_gather | solution.py:212
  205.1 15.5 %copy-start.1 = (bf16[128,64,128]{2,1,0:T(8,128)(2,1)S(1)}, bf16[128,64,128]{2,1,0:T(8,128)(2,1)}, u32[]{:S(2)}) copy-start(bf16[128,64,128]{2,1,0:T(8,128)(2,1)} %all-gather.14.cloned.1.call-done) | copy-start | bytes 6291460
  205.1 15.5 %copy-start.10 = (f32[16]{0:T(128)S(1)}, f32[16]{0:T(128)}, u32[]{:S(2)}) copy-start(f32[16]{0:T(128)} %copy-done.9) | copy-start | bytes 196
  205.1 15.5 %copy-start.13 = (f32[16]{0:T(128)S(1)}, f32[16]{0:T(128)}, u32[]{:S(2)}) copy-start(f32[16]{0:T(128)} %get-tuple-element.81) | copy-start | bytes 196
  220.6 3.2 copy-start.3
  220.6 3.2 copy-start.4
  220.6 3.2 copy-start.12
  220.6 3.2 copy-start.17
  226.0 99.8 %copy-start.6 = (f32[1024]{0:T(1024)S(1)}, f32[1024]{0:T(1024)}, u32[]{:S(2)}) copy-start(f32[1024]{0:T(1024)} %param.30) | copy-start | bytes 12292
  226.6 9.6 %all-to-all-start.1 = ((f32[8,1,256]{2,1,0:T(1,128)}), f32[8,1,256]{2,1,0:T(1,128)S(1)}, u32[]{:S(2)}, u32[]{:S(2)}) async-start(f32[8,1,256]{2,1,0:T(1,128)} %broadcast_in_dim.33), calls=%async_computation.1 | async-start | bytes 16384 | tf_op jit(solution)/shard_map/all_to_all | solution.py:29
  237.4 95.5 %all-to-all-start.3 = ((f32[32,1,1]{2,1,0:T(1,128)}), f32[32,1,1]{2,1,0:T(1,128)S(1)}, u32[]{:S(2)}, u32[]{:S(2)}) async-start(f32[32,1,1]{2,1,0:T(1,128)} %broadcast_in_dim.35), calls=%async_computation.3 | async-start | bytes 32768 | tf_op jit(solution)/shard_map/all_to_all | solution.py:29
  333.0 31.5 %all-to-all-start.2 = ((bf16[8,32,4096]{2,1,0:T(8,128)(2,1)}), bf16[8,32,4096]{2,1,0:T(8,128)(2,1)S(1)}, u32[]{:S(2)}, u32[]{:S(2)}) async-start(bf16[8,32,4096]{2,1,0:T(8,128)(2,1)} %bitcast.37), calls=%async_computation.2 | async-start | bytes 4194304 | tf_op jit(solution)/shard_map/all_to_all | solution.py:96
Sparse Core Ops, SparseCore 0:
  10.7 115.1 all-gather.7
  153.8 39.4 all-gather.13
  196.2 24.2 all-gather.9
  222.9 102.8 all-gather.11
where the time goes:
time: 375 us; the launch traced here: 372 us
  waiting for transfers between devices  248 us (66%)
  starting transfers between devices  29 us (8%)
  blocking collectives  24.6 us (7%)
  matrix products  22.6 us (6%)
  other arithmetic  19.1 us (5%)
  between operations  15.4 us (4%)
  local copies, waits for them, and re-layouts  13.2 us (4%)
    all_gather x1, waiting for transfers between devices, sent_together(): lax.all_gather(both, axis, axis=dim, tiled=True)  78.4 us
    all_gather x1, waiting for transfers between devices, local(): lax.all_gather(w_out, SEQ, axis=1, tiled=True)  77.9 us
    all_gather x2, waiting for transfers between devices, prefix_by_axis(): lax.all_gather(part.astype(kind), axis)  33.2 us
    all_to_all x3, waiting for transfers between devices, sent_to_all(): lax.all_to_all(jnp.broadcast_to(shard[None], (count, *shard.shape)), axis...  30.8 us
    all_to_all x1, waiting for transfers between devices, sent_and_summed(): lax.all_to_all(parts, axis, split_axis=0, concat_axis=0, tiled=True)  26.5 us
    all_to_all x3, starting transfers between devices, sent_to_all(): lax.all_to_all(jnp.broadcast_to(shard[None], (count, *shard.shape)), axis...  19.3 us
    unnamed x1, blocking collectives  16.5 us
    dot_general x3, matrix products, local(): jnp.dot(quant, weight_piece, preferred_element_type=jnp.float32)  10.7 us
  transfers between devices with their start and end apart: 10, of which 8 were waited for; matrix products, arithmetic and copies ran while one was open for 10% of the time, Pallas kernels for 0%

commit v1 on v0

--- a/solution.py
+++ b/solution.py
@@ -3,6 +3,8 @@
 from jax import lax
 from jax.sharding import Mesh
 from jax.sharding import PartitionSpec as P
+from jax.experimental import pallas as pl
+from jax.experimental.pallas import tpu as pltpu
 
 HEADS = 128
 HEAD_DIM = 64
@@ -10,8 +12,9 @@
 GROUPS = 8
 KERNEL = 4
 SPAN = 128
-SEQ = ("seq_0", "seq_1")
-SEQ_TENSOR = ("seq_0", "seq_1", "tensor")
+SEQ = ("x", "z")
+TENSOR = ("y", "c")
+SEQ_TENSOR = SEQ + TENSOR
 
 
 epsilon = 1e-05
@@ -109,6 +112,380 @@
     return (earlier[0] * later[0], later[0][:, None, None] * earlier[1] + later[1])
 
 
+MESH_ID = pl.DeviceIdType.MESH
+NX, NZ, NY, NC = (4, 8, 4, 2)
+CHUNKS = (384, 256, 256, 256, 256)
+X_ROWS = 1024
+
+
+def remote(src, dst, send_sem, recv_sem, where):
+    return pltpu.make_async_remote_copy(
+        src_ref=src,
+        dst_ref=dst,
+        send_sem=send_sem,
+        recv_sem=recv_sem,
+        device_id=where,
+        device_id_type=MESH_ID,
+    )
+
+
+def greet(peers):
+    barrier = pltpu.get_barrier_semaphore()
+    for peer in peers:
+        pl.semaphore_signal(barrier, inc=1, device_id=peer, device_id_type=MESH_ID)
+    pl.semaphore_wait(barrier, len(peers))
+
+
+def in_projection(
+    amax_ref,
+    hid_ref,
+    wx_ref,
+    wbd_ref,
+    x_out,
+    bc_out,
+    dt_out,
+    max_out,
+    rows,
+    quant,
+    w0,
+    w1,
+    w2,
+    w3,
+    w4,
+    stage,
+    r1,
+    r2,
+    own,
+    plus,
+    minus,
+    local_sem,
+    hx_send,
+    hx_recv,
+    hy_send,
+    hy_recv,
+    z_send,
+    z_recv,
+    rs_send,
+    rs_recv,
+):
+    x, z, y, c = (lax.axis_index(name) for name in ("x", "z", "y", "c"))
+    wbuf = (w0, w1, w2, w3, w4)
+
+    def at(dx=0, dz=0, dy=0, dc=0):
+        return (
+            lax.rem(x + dx + NX, NX),
+            lax.rem(z + dz + NZ, NZ),
+            lax.rem(y + dy + NY, NY),
+            lax.rem(c + dc, NC),
+        )
+
+    def z_rows(dz, low=0, count=128):
+        block = lax.rem(z + dz + NZ, NZ)
+        return pl.ds(pl.multiple_of(block * 128 + low, count), count)
+
+    def t_rows(dy, dc=0):
+        index = lax.rem(y + dy + NY, NY) * NC + lax.rem(c + dc, NC)
+        return pl.ds(pl.multiple_of(index * 32, 32), 32)
+
+    def x_of(r):
+        return lax.rem(x + r, NX)
+
+    local = []
+    for j in range(5):
+        src = wbd_ref if j == 0 else wx_ref.at[:, pl.ds(256 * (j - 1), 256)]
+        local.append(pltpu.make_async_copy(src, wbuf[j].at[z_rows(0)], local_sem.at[j]))
+    local.append(
+        pltpu.make_async_copy(
+            hid_ref.at[:, pl.ds(pl.multiple_of(x * X_ROWS, X_ROWS), X_ROWS)],
+            rows.at[x, t_rows(0)],
+            local_sem.at[5],
+        )
+    )
+    for copy in local:
+        copy.start()
+
+    greet(
+        [
+            at(dx=1),
+            at(dx=-1),
+            at(dx=2),
+            at(dz=1),
+            at(dz=-1),
+            at(dy=1),
+            at(dy=-1),
+            at(dc=1),
+        ]
+    )
+    for copy in local:
+        copy.wait()
+
+    sends = []
+
+    def go(copy):
+        copy.start()
+        sends.append(copy)
+
+    def z_copy(j, k, d):
+        sign = 1 if d == 0 else -1
+        if k < 3:
+            piece = z_rows(-sign * k)
+        else:
+            piece = z_rows(-sign * k, 64 * d, 64)
+        ref = wbuf[j].at[piece]
+        return remote(ref, ref, z_send.at[d, j, k], z_recv.at[d, j, k], at(dz=sign))
+
+    def z_arrived(j, k, d):
+        sign = 1 if d == 0 else -1
+        if k < 3:
+            piece = z_rows(-sign * (k + 1))
+        else:
+            piece = z_rows(-sign * (k + 1), 64 * d, 64)
+        ref = wbuf[j].at[piece]
+        remote(ref, ref, z_send.at[d, j, k], z_recv.at[d, j, k], at(dz=sign)).wait_recv()
+
+    def z_step(j, k):
+        for d in range(2):
+            if k > 0:
+                z_arrived(j, k - 1, d)
+            if k < 4:
+                go(z_copy(j, k, d))
+
+    def hx_copy(r):
+        dest = lax.rem(x + NX - r, NX)
+        src = hid_ref.at[:, pl.ds(pl.multiple_of(dest * X_ROWS, X_ROWS), X_ROWS)]
+        return remote(src, rows.at[x, t_rows(0)], hx_send.at[r], hx_recv.at[r], at(dx=-r))
+
+    def hx_arrived(r):
+        ref = rows.at[x_of(r), t_rows(0)]
+        remote(ref, ref, hx_send.at[r], hx_recv.at[r], at(dx=r)).wait_recv()
+
+    kind_place = {0: (-1, 0), 1: (1, 0), 2: (2, 0), 3: (0, 1), 4: (-1, 1), 5: (1, 1), 6: (2, 1)}
+
+    def hy_copy(r, kind, src_dy, where):
+        ref = rows.at[x_of(r), t_rows(src_dy)]
+        return remote(ref, ref, hy_send.at[r, kind], hy_recv.at[r, kind], where)
+
+    def hy_arrived(r, kind):
+        dy, dc = kind_place[kind]
+        ref = rows.at[x_of(r), t_rows(dy, dc)]
+        remote(ref, ref, hy_send.at[r, kind], hy_recv.at[r, kind], at(dc=1)).wait_recv()
+
+    def hy_first(r):
+        go(hy_copy(r, 0, 0, at(dy=1)))
+        go(hy_copy(r, 1, 0, at(dy=-1)))
+        go(hy_copy(r, 3, 0, at(dc=1)))
+
+    def hy_relay(r):
+        hy_arrived(r, 0)
+        if r in (0, 3):
+            go(hy_copy(r, 2, -1, at(dy=1)))
+        go(hy_copy(r, 4, -1, at(dc=1)))
+        hy_arrived(r, 1)
+        if r in (1, 2):
+            go(hy_copy(r, 2, 1, at(dy=-1)))
+        go(hy_copy(r, 5, 1, at(dc=1)))
+
+    def hy_last(r):
+        hy_arrived(r, 2)
+        go(hy_copy(r, 6, 2, at(dc=1)))
+
+    largest = jnp.zeros((8, 128), jnp.float32)
+    amax = jnp.full((8, 128), amax_ref[0], jnp.float32)
+    factor = (quant_range / amax)[0:1, 0:1]
+    in_scale = (amax / quant_range)[0:1, 0:1]
+    max_out[...] = largest
+
+    def quantized(r):
+        for kind in (3, 4, 5, 6):
+            hy_arrived(r, kind)
+        where = x_of(r)
+
+        def tile(i, carry):
+            part = pl.ds(pl.multiple_of(i * 32, 32), 32)
+            value = rows[where, part, :].astype(jnp.float32)
+            quant[where, part, :] = jnp.clip(
+                value * factor, -quant_range, quant_range
+            ).astype(jnp.bfloat16)
+            top = jnp.max(jnp.abs(value).reshape(4, 8, 1024), axis=0)
+            best = top[:, 0:128]
+            for lane in range(128, 1024, 128):
+                best = jnp.maximum(best, top[:, lane : lane + 128])
+            max_out[...] = jnp.maximum(max_out[...], best)
+            return carry
+
+        lax.fori_loop(0, 8, tile, 0)
+
+    starts = [0]
+    for width in CHUNKS:
+        starts.append(starts[-1] + width)
+
+    def cols(j):
+        return pl.ds(starts[j], CHUNKS[j])
+
+    def rs_copy(j, name):
+        slot, low, dst, dst_low, sign = {
+            "two_up": (0, 0, r1, 0, 1),
+            "two_down": (0, 128, r1, 128, -1),
+            "one_up_b": (1, 128, r2, 128, 1),
+            "one_down_a": (2, 0, r2, 256, -1),
+            "one_up_a": (1, 0, r2, 0, 1),
+            "one_down_b": (2, 128, r2, 384, -1),
+        }[name]
+        index = RS_NAMES.index(name)
+        return remote(
+            stage.at[slot, pl.ds(low, 128), cols(j)],
+            dst.at[pl.ds(dst_low, 128), cols(j)],
+            rs_send.at[j, index],
+            rs_recv.at[j, index],
+            at(dx=sign),
+        )
+
+    def product(j, r):
+        return jnp.dot(quant[x_of(r)], wbuf[j][...], preferred_element_type=jnp.float32)
+
+    def rs_multiply(j):
+        z_step(j, 4)
+        stage[0, :, cols(j)] = product(j, 2).astype(jnp.bfloat16)
+        value = product(j, 1)
+        plus[:, cols(j)] = value[0:128]
+        stage[1, 128:256, cols(j)] = value[128:256].astype(jnp.bfloat16)
+        go(rs_copy(j, "two_up"))
+        go(rs_copy(j, "two_down"))
+        value = product(j, 3)
+        minus[:, cols(j)] = value[128:256]
+        stage[2, 0:128, cols(j)] = value[0:128].astype(jnp.bfloat16)
+        go(rs_copy(j, "one_up_b"))
+        own[:, cols(j)] = product(j, 0)
+        go(rs_copy(j, "one_down_a"))
+
+    def rs_add(j):
+        rs_copy(j, "two_up").wait_recv()
+        stage[1, 0:128, cols(j)] = (
+            plus[:, cols(j)] + r1[0:128, cols(j)].astype(jnp.float32)
+        ).astype(jnp.bfloat16)
+        rs_copy(j, "two_down").wait_recv()
+        stage[2, 128:256, cols(j)] = (
+            minus[:, cols(j)] + r1[128:256, cols(j)].astype(jnp.float32)
+        ).astype(jnp.bfloat16)
+        go(rs_copy(j, "one_up_a"))
+        go(rs_copy(j, "one_down_b"))
+
+    def rs_final(j):
+        for name in ("one_up_b", "one_down_a", "one_up_a", "one_down_b"):
+            rs_copy(j, name).wait_recv()
+        total = (
+            own[:, cols(j)]
+            + r2[0:256, cols(j)].astype(jnp.float32)
+            + r2[256:512, cols(j)].astype(jnp.float32)
+        ) * in_scale
+        if j == 0:
+            bc_out[...] = total[:, 0:256].astype(jnp.bfloat16)
+            dt_out[...] = total[:, 256:384]
+        else:
+            x_out[:, 256 * (j - 1) : 256 * j] = total.astype(jnp.bfloat16)
+
+    z_step(0, 0)
+    for r in (1, 3, 2):
+        go(hx_copy(r))
+    hy_first(0)
+    z_step(1, 0)
+    for r in (1, 3):
+        hx_arrived(r)
+        hy_first(r)
+    z_step(0, 1)
+    hx_arrived(2)
+    hy_first(2)
+    z_step(2, 0)
+    hy_relay(0)
+    z_step(1, 1)
+    hy_relay(1)
+    z_step(0, 2)
+    z_step(3, 0)
+    hy_relay(3)
+    hy_relay(2)
+    hy_last(0)
+    hy_last(1)
+    z_step(2, 1)
+    z_step(1, 2)
+    hy_last(3)
+    hy_last(2)
+    z_step(0, 3)
+    z_step(4, 0)
+    z_step(3, 1)
+    for r in (0, 1, 3, 2):
+        quantized(r)
+    z_step(2, 2)
+    z_step(1, 3)
+    rs_multiply(0)
+    z_step(4, 1)
+    z_step(3, 2)
+    z_step(2, 3)
+    rs_multiply(1)
+    rs_add(0)
+    z_step(4, 2)
+    z_step(3, 3)
+    rs_multiply(2)
+    rs_add(1)
+    z_step(4, 3)
+    rs_final(0)
+    rs_multiply(3)
+    rs_add(2)
+    rs_final(1)
+    rs_multiply(4)
+    rs_add(3)
+    rs_final(2)
+    rs_add(4)
+    rs_final(3)
+    rs_final(4)
+    for copy in sends:
+        copy.wait_send()
+
+
+RS_NAMES = ("two_up", "two_down", "one_up_b", "one_down_a", "one_up_a", "one_down_b")
+
+
+def project_in(prev_amax, hidden_in, w_x, w_bc_dt):
+    total = sum(CHUNKS)
+    any_place = pl.BlockSpec(memory_space=pl.ANY)
+    vmem = pl.BlockSpec(memory_space=pltpu.VMEM)
+    dma = pltpu.SemaphoreType.DMA
+    return pl.pallas_call(
+        in_projection,
+        name="in_projection",
+        out_shape=(
+            jax.ShapeDtypeStruct((256, 1024), jnp.bfloat16),
+            jax.ShapeDtypeStruct((256, 256), jnp.bfloat16),
+            jax.ShapeDtypeStruct((256, 128), jnp.float32),
+            jax.ShapeDtypeStruct((8, 128), jnp.float32),
+        ),
+        in_specs=[pl.BlockSpec(memory_space=pltpu.SMEM), any_place, any_place, any_place],
+        out_specs=(vmem, vmem, vmem, vmem),
+        scratch_shapes=[
+            pltpu.VMEM((4, 256, X_ROWS), jnp.bfloat16),
+            pltpu.VMEM((4, 256, X_ROWS), jnp.bfloat16),
+            *[pltpu.VMEM((X_ROWS, width), jnp.bfloat16) for width in CHUNKS],
+            pltpu.VMEM((3, 256, total), jnp.bfloat16),
+            pltpu.VMEM((256, total), jnp.bfloat16),
+            pltpu.VMEM((512, total), jnp.bfloat16),
+            pltpu.VMEM((256, total), jnp.float32),
+            pltpu.VMEM((128, total), jnp.float32),
+            pltpu.VMEM((128, total), jnp.float32),
+            dma((6,)),
+            dma((4,)),
+            dma((4,)),
+            dma((4, 7)),
+            dma((4, 7)),
+            dma((2, 5, 4)),
+            dma((2, 5, 4)),
+            dma((5, 6)),
+            dma((5, 6)),
+        ],
+        compiler_params=pltpu.CompilerParams(
+            collective_id=0, has_side_effects=True, vmem_limit_bytes=48 * 2**20
+        ),
+    )(jnp.reshape(prev_amax, (1,)), hidden_in, w_x, w_bc_dt)
+
+
 def local(
     hidden_in,
     prev_amax,
@@ -127,25 +504,21 @@
     w_out,
 ):
     margin = KERNEL - 1
-    gathered = gather_directly(hidden_in, "tensor", 0)
-    abs_max = over_copies(jnp.max(jnp.abs(gathered.astype(jnp.float32))), SEQ)
-    in_scale = prev_amax / quant_range
     leading = lax.axis_index(SEQ) == 0
-    row_count = gathered.shape[0]
+    row_count = hidden_in.shape[0] * 8
     bc_width = w_bc.shape[1] * w_bc.shape[2] * w_bc.shape[3]
-    bc_rows = jnp.reshape(w_bc, (w_bc.shape[0], bc_width))
-    scaled = gathered.astype(jnp.float32) * (quant_range / prev_amax)
-    quant = jnp.clip(scaled, -quant_range, quant_range).astype(jnp.bfloat16)
-    pieces = sent_together((w_x, bc_rows, w_dt), SEQ, 0, 1)
-    x_proj, bc_proj, dt_proj = tuple(
-        (
-            jnp.dot(quant, weight_piece, preferred_element_type=jnp.float32)
-            for weight_piece in pieces
-        )
-    )
-    x_whole = (x_proj * in_scale).astype(jnp.bfloat16)
-    bc_whole = (bc_proj * in_scale).astype(jnp.bfloat16)
-    dt_raw = dt_proj * in_scale
+    heads = w_dt.shape[1]
+    w_bc_dt = jnp.concatenate(
+        [
+            jnp.reshape(w_bc, (w_bc.shape[0], bc_width)),
+            w_dt,
+            jnp.zeros((w_dt.shape[0], 128 - heads), w_dt.dtype),
+        ],
+        axis=1,
+    )
+    x_whole, bc_whole, dt_raw, top = project_in(prev_amax, hidden_in, w_x, w_bc_dt)
+    dt_raw = dt_raw[:, :heads]
+    abs_max = over_copies(jnp.max(top), SEQ)
     state_bc = jnp.reshape(conv_state_bc, (margin, bc_width))
     received = from_behind((x_whole[row_count - margin :], bc_whole[row_count - margin :]), SEQ, 1)
     x_edge = jnp.where(leading, conv_state_x, received[0])
@@ -205,37 +578,37 @@
     )
     ssm_out = local_part + carried_part + skip[None, None, :, None] * x_blocks.astype(jnp.float32)
     ssm_out = ssm_out.reshape(row_count, heads_here * HEAD_DIM)
-    squares = taken_together(jnp.sum(ssm_out * ssm_out, axis=1), "tensor")
+    squares = taken_together(jnp.sum(ssm_out * ssm_out, axis=1), TENSOR)
     mean_sq = squares / (HEADS * HEAD_DIM)
     normed = (ssm_out * lax.rsqrt(mean_sq + epsilon)[:, None] * norm_gain).astype(jnp.bfloat16)
     partial_out = jnp.dot(
         normed, lax.all_gather(w_out, SEQ, axis=1, tiled=True), preferred_element_type=jnp.float32
     )
-    layer_out = sent_and_summed(partial_out.astype(jnp.bfloat16), "tensor", 0).astype(jnp.bfloat16)
+    layer_out = sent_and_summed(partial_out.astype(jnp.bfloat16), TENSOR, 0).astype(jnp.bfloat16)
     return (layer_out, abs_max)
 
 
 def solution(mesh):
-    finer = Mesh(mesh.devices.reshape(4, 8, mesh.shape["tensor"]), ("seq_0", "seq_1", "tensor"))
+    finer = Mesh(mesh.devices.reshape(NX, NZ, NY, NC), SEQ_TENSOR)
     return jax.shard_map(
         local,
         mesh=finer,
         in_specs=(
             P(SEQ_TENSOR, None),
             P(),
-            P(SEQ, "tensor"),
-            P(SEQ, "tensor", None, None),
-            P(SEQ, "tensor"),
-            P(None, "tensor"),
-            P(None, "tensor", None, None),
-            P(None, "tensor"),
-            P(None, "tensor", None, None),
-            P("tensor"),
-            P("tensor"),
-            P("tensor"),
-            P("tensor", None, None),
-            P("tensor"),
-            P("tensor", SEQ),
+            P(SEQ, TENSOR),
+            P(SEQ, TENSOR, None, None),
+            P(SEQ, TENSOR),
+            P(None, TENSOR),
+            P(None, TENSOR, None, None),
+            P(None, TENSOR),
+            P(None, TENSOR, None, None),
+            P(TENSOR),
+            P(TENSOR),
+            P(TENSOR),
+            P(TENSOR, None, None),
+            P(TENSOR),
+            P(TENSOR, SEQ),
         ),
         out_specs=(P(SEQ_TENSOR, None), P()),
         check_vma=False,

time: 375 us -> 303 us (0.81)
  waiting for transfers between devices: 248 us -> 145 us
  Pallas kernels: 0 us -> 56 us
  matrix products: 22.6 us -> 11.9 us
  other arithmetic: 19.1 us -> 14 us
  starting transfers between devices: 29 us -> 24.6 us
    all_gather x1 -> x0, waiting for transfers between devices: 78.4 us -> none  [sent_together(): lax.all_gather(both, axis, axis=dim, tiled=True)]
    pallas_call x0 -> x1, Pallas kernels: none -> 56 us  [project_in(): pl.pallas_call(in_projection, name='in_projection', out_shape=(jax.ShapeD...]
    all_to_all x3 -> x2, waiting for transfers between devices: 30.8 us -> 3.9 us  [sent_to_all(): lax.all_to_all(jnp.broadcast_to(shard[None], (count, *shard.shape)), axis...]
    dot_general x3 -> x0, matrix products: 10.7 us -> none  [local(): jnp.dot(quant, weight_piece, preferred_element_type=jnp.float32)]
    all_to_all x3 -> x2, starting transfers between devices: 19.3 us -> 14.7 us  [sent_to_all(): lax.all_to_all(jnp.broadcast_to(shard[None], (count, *shard.shape)), axis...]
  transfers between devices with their start and end apart: 10 -> 8, of which waited for: 8 -> 6; matrix products, arithmetic and copies ran while one was open for 10% -> 8% of each run, Pallas kernels for 0% -> 0%
where the time goes in v1:
time: 303 us; the launch traced here: 300 us
  waiting for transfers between devices  145 us (48%)
  Pallas kernels  56 us (18%)
  starting transfers between devices  24.6 us (8%)
  blocking collectives  22.8 us (8%)
  between operations  15.4 us (5%)
  other arithmetic  14 us (5%)
  matrix products  11.9 us (4%)
  local copies, waits for them, and re-layouts  11 us (4%)
    all_gather x1, waiting for transfers between devices, local(): lax.all_gather(w_out, SEQ, axis=1, tiled=True)  78 us
    pallas_call x1, Pallas kernels, project_in(): pl.pallas_call(in_projection, name='in_projection', out_shape=(jax.ShapeD...  56 us
    all_gather x2, waiting for transfers between devices, prefix_by_axis(): lax.all_gather(part.astype(kind), axis)  32.7 us
    all_to_all x1, waiting for transfers between devices, sent_and_summed(): lax.all_to_all(parts, axis, split_axis=0, concat_axis=0, tiled=True)  26.5 us
    unnamed x1, blocking collectives  14.9 us
    all_to_all x2, starting transfers between devices, sent_to_all(): lax.all_to_all(jnp.broadcast_to(shard[None], (count, *shard.shape)), axis...  14.7 us
    all_gather x1, blocking collectives, prefix_by_axis(): lax.all_gather(part.astype(kind), axis)  7.88 us
    dot_general x1, matrix products, local(): jnp.dot(normed, lax.all_gather(w_out, SEQ, axis=1, tiled=True), preferred...  7.24 us
  transfers between devices with their start and end apart: 8, of which 6 were waited for; matrix products, arithmetic and copies ran while one was open for 8% of the time, Pallas kernels for 0%

profile of v1, /device:TPU:2, one launch (start us, length us, event | category | flops | bytes accessed | tf_op | source)
XLA Modules:
  0.0 300.3 jit_solution(2352233904817008674)
XLA Ops:
  7.3 0.9 copy.105
  9.7 0.9 copy-done
  10.6 0.9 copy-done.1
  11.6 56.0 %in_projection.1 = (bf16[256,1024]{1,0:T(8,128)(2,1)S(1)}, bf16[256,256]{1,0:T(8,128)(2,1)S(1)}, f32[256,128]{1,0:T(8,128)S(1)}, f32[8,128]{1,0:T(8,128)S(1)}) custom-call(f32[1]{0:T(128)} %bitcast.196.amax_ref, bf16[32,4096]{1,0:T(8,128)(2,1)S(1)} %copy-done, bf16[128,1024]{1,0:T(8,128)(2,1)S(1)} %copy-done.1, bf16[128,384]{1,0:T(8,128)(2,1)S(1)} %maximum_maximum_fusion.wbd_ref), custom_call_target="tpu_custom_call" | custom-call | tf_op jit(solution)/shard_map/in_projection/pallas_call | solution.py:452
  67.6 2.6 collective-permute-start
  70.2 2.9 collective-permute-start.1
  75.0 2.8 collective-permute-done.1
  78.1 0.8 fusion.73
  80.3 0.9 copy.83
  81.6 2.0 while.13
  81.6 0.9 bitcast_dynamic-update-slice_fusion.2
  82.7 0.9 bitcast_dynamic-update-slice_fusion.2
  83.7 0.8 add_convert_fusion
  86.1 14.9 %all-reduce = bf16[128]{0:T(256)(128)(2,1)S(1)} all-reduce(bf16[128]{0:T(256)(128)(2,1)S(1)} %dynamic-update-slice), channel_id=2, replica_groups=mesh['x'=4,'z'=8,'y'=4,'c'=2] {'z'}, use_global_device_ids=true, to_apply=%add | all-reduce | flops 128 | bytes 512
  101.2 20.4 %all-gather.11.cloned.1.call-done = bf16[128,64,128]{2,1,0:T(8,128)(2,1)} async-done(((bf16[16,64,128]{2,1,0:T(8,128)(2,1)}), bf16[128,64,128]{2,1,0:T(8,128)(2,1)}) %all-gather.11.cloned.1.call-update) | async-done | bytes 2097168 | tf_op jit(solution)/shard_map/all_gather | solution.py:73
  121.6 2.8 fusion.59
  125.2 7.9 %all-gather.2 = bf16[4,1,16]{2,1,0:T(2,128)(2,1)S(1)} all-gather(bf16[1,1,16]{2,1,0:T(2,128)(2,1)S(1)} %fusion.68), channel_id=1, replica_groups=mesh['x'=4,'z'=8,'y'=4,'c'=2] {'x'}, dimensions={0}, use_global_device_ids=true | all-gather | bytes 160 | tf_op jit(solution)/shard_map/all_gather | solution.py:73
  133.3 1.1 copy.107
  134.6 1.9 convolution_bitcast_fusion.1
  136.5 12.3 %all-gather.7.cloned.1.call-done = bf16[4,16,64,128]{3,2,1,0:T(8,128)(2,1)} async-done(((bf16[1,16,64,128]{3,2,1,0:T(8,128)(2,1)}), bf16[4,16,64,128]{3,2,1,0:T(8,128)(2,1)}) %all-gather.7.cloned.1.call-update) | async-done | bytes 1048592 | tf_op jit(solution)/shard_map/all_gather | solution.py:73
  148.8 3.1 %fusion.25 = f32[16,64,128]{2,1,0:T(8,128)S(1)} fusion(f32[16,64,128]{2,1,0:T(8,128)S(1)} %copy-done.3, bf16[4,16,64,128]{3,2,1,0:T(8,128)(2,1)} %all-gather.7.cloned.1.call-done, f32[16]{0:T(128)S(1)} %get-tuple-element.88, f32[16]{0:T(128)S(1)} %get-tuple-element.96, f32[16]{0:T(128)S(1)} %get-tuple-element.95, f32[16]{0:T(128)S(1)} %get-tuple-element.94, ...), kind=kLoop, calls=%fused_computation.55 | loop fusion | flops 6422528 | bytes 4195149 | tf_op jit(solution)/shard_map/jit(_where)/select_n | solution.py:571
  152.0 2.2 multiply_reduce_fusion
  154.8 4.3 %all-to-all-start = ((f32[8,1,256]{2,1,0:T(1,128)}), f32[8,1,256]{2,1,0:T(1,128)S(1)}, u32[]{:S(2)}, u32[]{:S(2)}) async-start(f32[8,1,256]{2,1,0:T(1,128)} %broadcast_in_dim.34), calls=%async_computation | async-start | bytes 16384 | tf_op jit(solution)/shard_map/all_to_all | solution.py:32
  159.7 0.8 copy.87
  160.5 3.9 %all-to-all-done = f32[8,1,256]{2,1,0:T(1,128)S(1)} async-done(((f32[8,1,256]{2,1,0:T(1,128)}), f32[8,1,256]{2,1,0:T(1,128)S(1)}, u32[]{:S(2)}, u32[]{:S(2)}) %all-to-all-start) | async-done | bytes 8224 | tf_op jit(solution)/shard_map/all_to_all | solution.py:32
  164.4 1.3 broadcast_in_dim.35
  165.6 10.4 %all-to-all-start.2 = ((f32[32,1,1]{2,1,0:T(1,128)}), f32[32,1,1]{2,1,0:T(1,128)S(1)}, u32[]{:S(2)}, u32[]{:S(2)}) async-start(f32[32,1,1]{2,1,0:T(1,128)} %broadcast_in_dim.35), calls=%async_computation.2 | async-start | bytes 32768 | tf_op jit(solution)/shard_map/all_to_all | solution.py:32
  176.1 78.0 %all-gather.9.cloned.1.call-done = bf16[1024,4096]{1,0:T(8,128)(2,1)} async-done(((bf16[1024,128]{1,0:T(8,128)(2,1)}), bf16[1024,4096]{1,0:T(8,128)(2,1)}) %all-gather.9.cloned.1.call-update) | async-done | bytes 8388624 | tf_op jit(solution)/shard_map/all_gather | solution.py:585
  254.0 7.2 %convolution_convert_fusion = bf16[256,4096]{1,0:T(8,128)(2,1)} fusion(bf16[1024,4096]{1,0:T(8,128)(2,1)} %all-gather.9.cloned.1.call-done, f32[128,8,2,128]{3,2,1,0:T(2,128)S(1)} %bitcast.197, f32[1024]{0:T(1024)S(1)} %copy-done.6, f32[256]{0:T(256)S(1)} %add_rsqrt_fusion), kind=kOutput, calls=%fused_computation.4 | convolution fusion | flops 2149318656 | bytes 11539456 | tf_op jit(solution)/shard_map/dot_general | solution.py:584
  261.3 4.3 %all-to-all-start.1 = ((bf16[8,32,4096]{2,1,0:T(8,128)(2,1)}), bf16[8,32,4096]{2,1,0:T(8,128)(2,1)S(1)}, u32[]{:S(2)}, u32[]{:S(2)}) async-start(bf16[8,32,4096]{2,1,0:T(8,128)(2,1)} %bitcast.38), calls=%async_computation.1 | async-start | bytes 4194304 | tf_op jit(solution)/shard_map/all_to_all | solution.py:99
  266.2 26.5 %all-to-all-done.1 = bf16[8,32,4096]{2,1,0:T(8,128)(2,1)S(1)} async-done(((bf16[8,32,4096]{2,1,0:T(8,128)(2,1)}), bf16[8,32,4096]{2,1,0:T(8,128)(2,1)S(1)}, u32[]{:S(2)}, u32[]{:S(2)}) %all-to-all-start.1) | async-done | bytes 2097184 | tf_op jit(solution)/shard_map/all_to_all | solution.py:99
  292.8 1.1 reduce_sum.42
  (81 shorter events, 9.2 us)
Async XLA Ops:
  7.2 67.7 %copy-start.7 = (f32[4,1024]{1,0:T(4,128)S(1)}, f32[4,1024]{1,0:T(4,128)}, u32[]{:S(2)}) copy-start(f32[4,1024]{1,0:T(4,128)} %param.22) | copy-start | bytes 49156
  7.2 67.7 %copy-start.9 = (f32[4,1,2,128]{3,2,1,0:T(2,128)S(1)}, f32[4,1,2,128]{3,2,1,0:T(2,128)}, u32[]{:S(2)}) copy-start(f32[4,1,2,128]{3,2,1,0:T(2,128)} %param.23) | copy-start | bytes 12292
  7.2 70.6 %copy-start.10 = (bf16[3,1,2,128]{3,2,1,0:T(2,128)(2,1)S(1)}, bf16[3,1,2,128]{3,2,1,0:T(2,128)(2,1)}, u32[]{:S(2)}) copy-start(bf16[3,1,2,128]{3,2,1,0:T(2,128)(2,1)} %param.25) | copy-start | bytes 4612
  7.2 71.7 %copy-start.8 = (bf16[3,1024]{1,0:T(4,128)(2,1)S(1)}, bf16[3,1024]{1,0:T(4,128)(2,1)}, u32[]{:S(2)}) copy-start(bf16[3,1024]{1,0:T(4,128)(2,1)} %param.24) | copy-start | bytes 18436
  7.2 114.4 %all-gather.11.cloned.1.call-start = ((), (), s32[]{:S(2)}) async-start(), calls=%async_computation.5 | async-start | bytes 2359296 | tf_op jit(solution)/shard_map/all_gather | solution.py:73
  9.7 1.0 copy-start
  10.6 0.9 copy-start.1
  67.6 11.3 %collective-permute-start = (bf16[3,1024]{1,0:T(4,128)(2,1)S(1)}, bf16[3,1024]{1,0:T(4,128)(2,1)S(1)}, u32[]{:S(2)}, u32[]{:S(2)}) collective-permute-start(bf16[3,1024]{1,0:T(4,128)(2,1)S(1)} %slice.137), channel_id=1, source_target_pairs={{0,8},{8,16},{16,24},{24,32},{32,40},{40,48},{48,56},{56,64},{64,7... | collective-permute-start | bytes 18440 | tf_op jit(solution)/shard_map/ppermute | solution.py:58
  70.2 7.6 %collective-permute-start.1 = (bf16[3,256]{1,0:T(4,128)(2,1)S(1)}, bf16[3,256]{1,0:T(4,128)(2,1)S(1)}, u32[]{:S(2)}, u32[]{:S(2)}) collective-permute-start(bf16[3,256]{1,0:T(4,128)(2,1)S(1)} %slice.145), channel_id=1, source_target_pairs={{0,8},{8,16},{16,24},{24,32},{32,40},{40,48},{48,56},{56,64},{64,7... | collective-permute-start | bytes 4616 | tf_op jit(solution)/shard_map/ppermute | solution.py:58
  81.6 2.1 copy-start.3
  81.6 3.0 %copy-start.12 = (u32[256]{0:T(256)S(1)}, u32[256]{0:T(256)}, u32[]{:S(2)}) copy-start(u32[256]{0:T(256)} %constant.75) | copy-start | bytes 3076
  84.5 64.2 %all-gather.7.cloned.1.call-start = ((), (), s32[]{:S(2)}) async-start(), calls=%async_computation.3 | async-start | bytes 1310720 | tf_op jit(solution)/shard_map/all_gather | solution.py:73
  124.4 129.7 %all-gather.9.cloned.1.call-start = ((), (), s32[]{:S(2)}) async-start(), calls=%async_computation.4 | async-start | bytes 8650752 | tf_op jit(solution)/shard_map/all_gather | solution.py:585
  133.3 15.5 %copy-start.2 = (bf16[128,64,128]{2,1,0:T(8,128)(2,1)S(1)}, bf16[128,64,128]{2,1,0:T(8,128)(2,1)}, u32[]{:S(2)}) copy-start(bf16[128,64,128]{2,1,0:T(8,128)(2,1)} %all-gather.11.cloned.1.call-done) | copy-start | bytes 6291460
  148.8 3.2 %copy-start.4 = (f32[2,16,64,128]{3,2,1,0:T(8,128)S(1)}, f32[2,16,64,128]{3,2,1,0:T(8,128)}, u32[]{:S(2)}) copy-start(f32[2,16,64,128]{3,2,1,0:T(8,128)} %get-tuple-element.37) | copy-start | bytes 3145732
  148.8 3.2 %copy-start.5 = (f32[2,128,16,64]{1,3,2,0:T(8,128)S(1)}, f32[2,128,16,64]{1,3,2,0:T(8,128)}, u32[]{:S(2)}) copy-start(f32[2,128,16,64]{1,3,2,0:T(8,128)} %convolution_bitcast_fusion.1) | copy-start | bytes 3145732
  148.8 3.2 %copy-start.11 = (f32[16]{0:T(128)S(1)}, f32[16]{0:T(128)}, u32[]{:S(2)}) copy-start(f32[16]{0:T(128)} %param.28) | copy-start | bytes 196
  154.2 99.9 %copy-start.6 = (f32[1024]{0:T(1024)S(1)}, f32[1024]{0:T(1024)}, u32[]{:S(2)}) copy-start(f32[1024]{0:T(1024)} %param.30) | copy-start | bytes 12292
  154.8 9.6 %all-to-all-start = ((f32[8,1,256]{2,1,0:T(1,128)}), f32[8,1,256]{2,1,0:T(1,128)S(1)}, u32[]{:S(2)}, u32[]{:S(2)}) async-start(f32[8,1,256]{2,1,0:T(1,128)} %broadcast_in_dim.34), calls=%async_computation | async-start | bytes 16384 | tf_op jit(solution)/shard_map/all_to_all | solution.py:32
  165.6 95.6 %all-to-all-start.2 = ((f32[32,1,1]{2,1,0:T(1,128)}), f32[32,1,1]{2,1,0:T(1,128)S(1)}, u32[]{:S(2)}, u32[]{:S(2)}) async-start(f32[32,1,1]{2,1,0:T(1,128)} %broadcast_in_dim.35), calls=%async_computation.2 | async-start | bytes 32768 | tf_op jit(solution)/shard_map/all_to_all | solution.py:32
  261.3 31.5 %all-to-all-start.1 = ((bf16[8,32,4096]{2,1,0:T(8,128)(2,1)}), bf16[8,32,4096]{2,1,0:T(8,128)(2,1)S(1)}, u32[]{:S(2)}, u32[]{:S(2)}) async-start(bf16[8,32,4096]{2,1,0:T(8,128)(2,1)} %bitcast.38), calls=%async_computation.1 | async-start | bytes 4194304 | tf_op jit(solution)/shard_map/all_to_all | solution.py:99
Sparse Core Ops, SparseCore 0:
  84.7 36.8 all-gather.10
  124.5 24.2 all-gather.6
  151.2 102.7 all-gather.8

commit v2 on v1

--- a/solution.py
+++ b/solution.py
@@ -486,6 +486,330 @@
     )(jnp.reshape(prev_amax, (1,)), hidden_in, w_x, w_bc_dt)
 
 
+GROUP_SLOTS = ((0, 4), (-1, 1), (-2, 2), (-3, 3))
+GROUP_ORDER = (1, 2, 3, 0)
+Y_NAMES = ("two_up", "two_down", "one_up_b", "one_down_a", "one_up_a", "one_down_b")
+
+
+def out_projection(
+    u_ref,
+    sq_ref,
+    w_ref,
+    out_ref,
+    tokens,
+    weights,
+    partial,
+    from_core,
+    ystage,
+    ry1,
+    ry2,
+    yown,
+    yup,
+    ydown,
+    fstage,
+    landed,
+    squares,
+    local_sem,
+    x_send,
+    x_recv,
+    z_send,
+    z_recv,
+    sq_send,
+    sq_recv,
+    c_send,
+    c_recv,
+    y_send,
+    y_recv,
+    f_send,
+    f_recv,
+):
+    x, z, y, c = (lax.axis_index(name) for name in ("x", "z", "y", "c"))
+
+    def at(dx=0, dz=0, dy=0, dc=0):
+        return (
+            lax.rem(x + dx + NX, NX),
+            lax.rem(z + dz + NZ, NZ),
+            lax.rem(y + dy + NY, NY),
+            lax.rem(c + dc, NC),
+        )
+
+    def x_of(dx):
+        return lax.rem(x + dx + NX, NX)
+
+    def y_of(dy):
+        return lax.rem(y + dy + NY, NY)
+
+    def z_cols(slot):
+        for g, pair in enumerate(GROUP_SLOTS):
+            if slot in pair:
+                return pl.ds(256 * g + 128 * pair.index(slot), 128)
+
+    mine = pltpu.make_async_copy(w_ref, weights.at[:, z_cols(0)], local_sem.at[0])
+    mine.start()
+    mine_u = pltpu.make_async_copy(u_ref, tokens.at[x], local_sem.at[1])
+    mine_u.start()
+    greet(
+        [at(dx=1), at(dx=-1), at(dx=2), at(dz=1), at(dz=-1)]
+        + [at(dy=dy, dc=dc) for dy in range(4) for dc in range(2) if (dy, dc) != (0, 0)]
+    )
+    mine.wait()
+    mine_u.wait()
+
+    sends = []
+
+    def go(copy):
+        copy.start()
+        sends.append(copy)
+
+    def x_copy(p, kind, source, where):
+        ref = tokens.at[x_of(source), pl.ds(64 * p, 64)]
+        return remote(ref, ref, x_send.at[p, kind], x_recv.at[p, kind], where)
+
+    def x_arrived(p, kind):
+        x_copy(p, kind, {0: -1, 1: 1, 2: 2}[kind], at(dx=1)).wait_recv()
+
+    def x_relay_up(p):
+        x_arrived(p, 0)
+        go(x_copy(p, 2, -1, at(dx=1)))
+
+    def x_relay_down(p):
+        x_arrived(p, 1)
+        go(x_copy(p, 2, 1, at(dx=-1)))
+
+    def z_copy(j, k, d):
+        sign = 1 if d == 0 else -1
+        rows = pl.ds(256 * j, 256)
+        arrives = -sign * (k + 1)
+        if k == 3:
+            arrives = 4
+        return remote(
+            weights.at[rows, z_cols(-sign * k)],
+            weights.at[rows, z_cols(arrives)],
+            z_send.at[d, j, k],
+            z_recv.at[d, j, k],
+            at(dz=sign),
+        )
+
+    def z_step(j, k, d):
+        if k > 0:
+            z_copy(j, k - 1, d).wait_recv()
+        if k < 3 or j // 2 == d:
+            go(z_copy(j, k, d))
+
+    others = [(dy, dc) for dy in range(4) for dc in range(2) if (dy, dc) != (0, 0)]
+
+    def t_index(dy, dc):
+        return y_of(dy) * NC + lax.rem(c + dc, NC)
+
+    def sq_copy(n):
+        dy, dc = others[n]
+        there = pl.ds(pl.multiple_of(t_index(dy, dc) * 32, 32), 32)
+        return remote(
+            sq_ref.at[there], squares.at[n], sq_send.at[n], sq_recv.at[n], at(dy=dy, dc=dc)
+        )
+
+    for p in (0, 1, 2, 3):
+        go(x_copy(p, 0, 0, at(dx=1)))
+        go(x_copy((p + 2) % 4, 1, 0, at(dx=-1)))
+        for d in range(2):
+            z_step(p, 0, d)
+    for n in range(7):
+        go(sq_copy(n))
+    z_step(0, 1, 0), z_step(0, 1, 1), z_step(1, 1, 0), z_step(1, 1, 1)
+    x_relay_up(0), x_relay_down(2)
+    z_step(2, 1, 0), z_step(2, 1, 1), z_step(3, 1, 0), z_step(3, 1, 1)
+    x_relay_up(1), x_relay_down(3)
+    for j in range(4):
+        z_step(j, 2, 0), z_step(j, 2, 1)
+    for p in (2, 3):
+        x_arrived(p, 0), x_arrived((p + 2) % 4, 1)
+    for p in range(4):
+        x_arrived(p, 2)
+
+    def cols(g):
+        return pl.ds(256 * g, 256)
+
+    def multiply(g):
+        def one(slot, carry):
+            value = jnp.dot(
+                tokens[slot], weights[:, cols(g)], preferred_element_type=jnp.float32
+            ).astype(jnp.bfloat16)
+            value = value.reshape(NY, NC, 32, 256)
+            for core in range(NC):
+                partial[g, core, :, slot] = value[:, core]
+            return carry
+
+        lax.fori_loop(0, NX, one, 0)
+
+    def c_copy(g):
+        other = lax.rem(c + 1, NC)
+        return remote(
+            partial.at[g, other], from_core.at[g], c_send.at[g], c_recv.at[g], at(dc=1)
+        )
+
+    def y_copy(g, name):
+        slot, low, dst, sign = {
+            "two_up": (2, 0, ry1.at[g], 1),
+            "two_down": (2, 2, ry1.at[g], -1),
+            "one_up_b": (1, 2, ry2.at[g, 0], 1),
+            "one_down_a": (3, 0, ry2.at[g, 1], -1),
+            "one_up_a": (1, 0, ry2.at[g, 0], 1),
+            "one_down_b": (3, 2, ry2.at[g, 1], -1),
+        }[name]
+        index = Y_NAMES.index(name)
+        return remote(
+            ystage.at[g, slot, pl.ds(low, 2)],
+            dst.at[pl.ds(low, 2)],
+            y_send.at[g, index],
+            y_recv.at[g, index],
+            at(dy=sign),
+        )
+
+    def both_cores(g, dy):
+        where = y_of(dy)
+        return partial[g, c, where].astype(jnp.float32) + from_core[g, where].astype(jnp.float32)
+
+    def y_first(g):
+        c_copy(g).wait_recv()
+        ystage[g, 2] = both_cores(g, 2).astype(jnp.bfloat16)
+        value = both_cores(g, 1)
+        yup[g] = value[0:2]
+        ystage[g, 1, 2:4] = value[2:4].astype(jnp.bfloat16)
+        go(y_copy(g, "two_up"))
+        go(y_copy(g, "two_down"))
+        value = both_cores(g, 3)
+        ydown[g] = value[2:4]
+        ystage[g, 3, 0:2] = value[0:2].astype(jnp.bfloat16)
+        go(y_copy(g, "one_up_b"))
+        yown[g] = both_cores(g, 0)
+        go(y_copy(g, "one_down_a"))
+
+    def y_add(g):
+        y_copy(g, "two_up").wait_recv()
+        ystage[g, 1, 0:2] = (yup[g] + ry1[g, 0:2].astype(jnp.float32)).astype(jnp.bfloat16)
+        y_copy(g, "two_down").wait_recv()
+        ystage[g, 3, 2:4] = (ydown[g] + ry1[g, 2:4].astype(jnp.float32)).astype(jnp.bfloat16)
+        go(y_copy(g, "one_up_a"))
+        go(y_copy(g, "one_down_b"))
+
+    def out_cols(x_slot, g, side):
+        block = lax.rem(z + GROUP_SLOTS[g][side] + NZ, NZ)
+        return pl.ds(pl.multiple_of(x_slot * 1024 + block * 128, 128), 128)
+
+    def f_copy(g, side, dx):
+        return remote(
+            fstage.at[g, x_of(dx), :, pl.ds(128 * side, 128)],
+            landed.at[:, out_cols(x, g, side)],
+            f_send.at[g, side, dx],
+            f_recv.at[g, side, dx],
+            at(dx=dx),
+        )
+
+    def f_arrived(g, side, dx):
+        ref = landed.at[:, out_cols(x_of(-dx), g, side)]
+        remote(
+            ref, ref, f_send.at[g, side, dx], f_recv.at[g, side, dx], at(dx=-dx)
+        ).wait_recv()
+
+    def y_final(g):
+        for name in ("one_up_b", "one_down_a", "one_up_a", "one_down_b"):
+            y_copy(g, name).wait_recv()
+        fstage[g] = (
+            yown[g] + ry2[g, 0].astype(jnp.float32) + ry2[g, 1].astype(jnp.float32)
+        ).astype(jnp.bfloat16)
+        here = fstage[g, x]
+        for side in range(2):
+            landed[:, out_cols(x, g, side)] = here[:, 128 * side : 128 * side + 128]
+        for dx in (2, 1, 3):
+            for side in range(2):
+                go(f_copy(g, side, dx))
+
+    multiply(1)
+    go(c_copy(1))
+    for j in range(4):
+        z_step(j, 3, 0), z_step(j, 3, 1)
+    multiply(2)
+    go(c_copy(2))
+    y_first(1)
+    multiply(3)
+    go(c_copy(3))
+    y_first(2)
+    y_add(1)
+    for j in range(4):
+        z_copy(j, 3, j // 2).wait_recv()
+    multiply(0)
+    go(c_copy(0))
+    y_first(3)
+    y_add(2)
+    y_final(1)
+    y_first(0)
+    y_add(3)
+    y_final(2)
+    y_add(0)
+    y_final(3)
+
+    total = sq_ref[pl.ds(pl.multiple_of(t_index(0, 0) * 32, 32), 32), :]
+    for n in range(7):
+        sq_copy(n).wait_recv()
+        total = total + squares[n]
+    mean_sq = jnp.sum(total, axis=1, keepdims=True) / (HEADS * HEAD_DIM)
+    scale = lax.rsqrt(mean_sq + epsilon)
+
+    y_final(0)
+    for g in GROUP_ORDER:
+        for dx in (1, 2, 3):
+            for side in range(2):
+                f_arrived(g, side, dx)
+    out_ref[...] = (landed[...].astype(jnp.float32) * scale).astype(jnp.bfloat16)
+    for copy in sends:
+        copy.wait_send()
+
+
+def project_out(u, squares, w_out):
+    any_place = pl.BlockSpec(memory_space=pl.ANY)
+    vmem = pl.BlockSpec(memory_space=pltpu.VMEM)
+    dma = pltpu.SemaphoreType.DMA
+    bf16, f32 = (jnp.bfloat16, jnp.float32)
+    return pl.pallas_call(
+        out_projection,
+        name="out_projection",
+        out_shape=jax.ShapeDtypeStruct((32, 4096), bf16),
+        in_specs=[any_place, vmem, any_place],
+        out_specs=vmem,
+        scratch_shapes=[
+            pltpu.VMEM((4, 256, 1024), bf16),
+            pltpu.VMEM((1024, 1024), bf16),
+            pltpu.VMEM((4, 2, 4, 4, 32, 256), bf16),
+            pltpu.VMEM((4, 4, 4, 32, 256), bf16),
+            pltpu.VMEM((4, 4, 4, 32, 256), bf16),
+            pltpu.VMEM((4, 4, 32, 256), bf16),
+            pltpu.VMEM((4, 2, 4, 32, 256), bf16),
+            pltpu.VMEM((4, 4, 32, 256), f32),
+            pltpu.VMEM((4, 2, 32, 256), f32),
+            pltpu.VMEM((4, 2, 32, 256), f32),
+            pltpu.VMEM((4, 4, 32, 256), bf16),
+            pltpu.VMEM((32, 4096), bf16),
+            pltpu.VMEM((7, 32, 128), f32),
+            dma((2,)),
+            dma((4, 3)),
+            dma((4, 3)),
+            dma((2, 4, 4)),
+            dma((2, 4, 4)),
+            dma((7,)),
+            dma((7,)),
+            dma((4,)),
+            dma((4,)),
+            dma((4, 6)),
+            dma((4, 6)),
+            dma((4, 2, 4)),
+            dma((4, 2, 4)),
+        ],
+        compiler_params=pltpu.CompilerParams(
+            collective_id=1, has_side_effects=True, vmem_limit_bytes=48 * 2**20
+        ),
+    )(u, squares, w_out)
+
+
 def local(
     hidden_in,
     prev_amax,
@@ -578,13 +902,9 @@
     )
     ssm_out = local_part + carried_part + skip[None, None, :, None] * x_blocks.astype(jnp.float32)
     ssm_out = ssm_out.reshape(row_count, heads_here * HEAD_DIM)
-    squares = taken_together(jnp.sum(ssm_out * ssm_out, axis=1), TENSOR)
-    mean_sq = squares / (HEADS * HEAD_DIM)
-    normed = (ssm_out * lax.rsqrt(mean_sq + epsilon)[:, None] * norm_gain).astype(jnp.bfloat16)
-    partial_out = jnp.dot(
-        normed, lax.all_gather(w_out, SEQ, axis=1, tiled=True), preferred_element_type=jnp.float32
-    )
-    layer_out = sent_and_summed(partial_out.astype(jnp.bfloat16), TENSOR, 0).astype(jnp.bfloat16)
+    squares = jnp.sum((ssm_out * ssm_out).reshape(row_count, -1, 128), axis=1)
+    scaled_out = (ssm_out * norm_gain).astype(jnp.bfloat16)
+    layer_out = project_out(scaled_out, squares, w_out)
     return (layer_out, abs_max)
 
 

time: 303 us -> 216 us (0.71)
  waiting for transfers between devices: 145 us -> 26.8 us
  Pallas kernels: 56 us -> 103 us
  starting transfers between devices: 24.6 us -> 13.2 us
  matrix products: 11.9 us -> 6.02 us
  local copies, waits for them, and re-layouts: 11 us -> 14.9 us
    all_gather x1 -> x0, waiting for transfers between devices: 78 us -> none  [local(): lax.all_gather(w_out, SEQ, axis=1, tiled=True)]
    pallas_call x0 -> x1, Pallas kernels: none -> 47 us  [project_out(): pl.pallas_call(out_projection, name='out_projection', out_shape=jax.Shape...]
    all_to_all x1 -> x0, waiting for transfers between devices: 26.5 us -> none  [sent_and_summed(): lax.all_to_all(parts, axis, split_axis=0, concat_axis=0, tiled=True)]
    all_gather x2, waiting for transfers between devices: 32.7 us -> 23.6 us  [prefix_by_axis(): lax.all_gather(part.astype(kind), axis)]
    dot_general x1 -> x0, matrix products: 7.24 us -> none  [local(): jnp.dot(normed, lax.all_gather(w_out, SEQ, axis=1, tiled=True), preferred...]
    all_to_all x2 -> x1, starting transfers between devices: 14.7 us -> 7.58 us  [sent_to_all(): lax.all_to_all(jnp.broadcast_to(shard[None], (count, *shard.shape)), axis...]
    all_to_all x1 -> x0, starting transfers between devices: 4.29 us -> none  [sent_and_summed(): lax.all_to_all(parts, axis, split_axis=0, concat_axis=0, tiled=True)]
    all_to_all x2 -> x1, waiting for transfers between devices: 3.9 us -> 0.34 us  [sent_to_all(): lax.all_to_all(jnp.broadcast_to(shard[None], (count, *shard.shape)), axis...]
  transfers between devices with their start and end apart: 8 -> 5, of which waited for: 6 -> 4; matrix products, arithmetic and copies ran while one was open for 8% -> 4% of each run, Pallas kernels for 0% -> 0%
where the time goes in v2:
time: 216 us
  Pallas kernels  103 us (48%)
  waiting for transfers between devices  26.8 us (12%)
  blocking collectives  22.9 us (11%)
  between operations  15.8 us (7%)
  local copies, waits for them, and re-layouts  14.9 us (7%)
  starting transfers between devices  13.2 us (6%)
  other arithmetic  13 us (6%)
  matrix products  6.02 us (3%)
    pallas_call x1, Pallas kernels, project_in(): pl.pallas_call(in_projection, name='in_projection', out_shape=(jax.ShapeD...  56 us
    pallas_call x1, Pallas kernels, project_out(): pl.pallas_call(out_projection, name='out_projection', out_shape=jax.Shape...  47 us
    all_gather x2, waiting for transfers between devices, prefix_by_axis(): lax.all_gather(part.astype(kind), axis)  23.6 us
    unnamed x1, blocking collectives  14.9 us
    all_gather x1, blocking collectives, prefix_by_axis(): lax.all_gather(part.astype(kind), axis)  8.01 us
    all_to_all x1, starting transfers between devices, sent_to_all(): lax.all_to_all(jnp.broadcast_to(shard[None], (count, *shard.shape)), axis...  7.58 us
    ppermute x2, starting transfers between devices, from_behind(): lax.ppermute(value, axis, [(source, source + steps) for source in range(f...  5.5 us
    unnamed x38, local copies, waits for them, and re-layouts  5.17 us
  transfers between devices with their start and end apart: 5, of which 4 were waited for; matrix products, arithmetic and copies ran while one was open for 4% of the time, Pallas kernels for 0%

profile of v2, /device:TPU:2, one launch (start us, length us, event | category | flops | bytes accessed | tf_op | source)
XLA Modules:
  0.0 215.7 jit_solution(3752766267956633489)
XLA Ops:
  7.3 0.9 copy.116
  8.1 0.8 copy.86
  9.7 0.9 copy-done
  10.6 0.9 copy-done.1
  11.6 56.0 %in_projection.1 = (bf16[256,1024]{1,0:T(8,128)(2,1)S(1)}, bf16[256,256]{1,0:T(8,128)(2,1)S(1)}, f32[256,128]{1,0:T(8,128)S(1)}, f32[8,128]{1,0:T(8,128)S(1)}) custom-call(f32[1]{0:T(128)} %bitcast.186.amax_ref, bf16[32,4096]{1,0:T(8,128)(2,1)S(1)} %copy-done, bf16[128,1024]{1,0:T(8,128)(2,1)S(1)} %copy-done.1, bf16[128,384]{1,0:T(8,128)(2,1)S(1)} %maximum_maximum_fusion.wbd_ref), custom_call_target="tpu_custom_call" | custom-call | tf_op jit(solution)/shard_map/in_projection/pallas_call | solution.py:452
  67.6 2.6 %collective-permute-start = (bf16[3,1024]{1,0:T(4,128)(2,1)S(1)}, bf16[3,1024]{1,0:T(4,128)(2,1)S(1)}, u32[]{:S(2)}, u32[]{:S(2)}) collective-permute-start(bf16[3,1024]{1,0:T(4,128)(2,1)S(1)} %slice.137), channel_id=1, source_target_pairs={{0,8},{8,16},{16,24},{24,32},{32,40},{40,48},{48,56},{56,64},{64,7... | collective-permute-start | bytes 18440 | tf_op jit(solution)/shard_map/ppermute | solution.py:58
  70.2 2.9 %collective-permute-start.1 = (bf16[3,256]{1,0:T(4,128)(2,1)S(1)}, bf16[3,256]{1,0:T(4,128)(2,1)S(1)}, u32[]{:S(2)}, u32[]{:S(2)}) collective-permute-start(bf16[3,256]{1,0:T(4,128)(2,1)S(1)} %slice.145), channel_id=1, source_target_pairs={{0,8},{8,16},{16,24},{24,32},{32,40},{40,48},{48,56},{56,64},{64,7... | collective-permute-start | bytes 4616 | tf_op jit(solution)/shard_map/ppermute | solution.py:58
  73.1 0.7 compare_select_fusion
  73.9 0.7 negate_multiply_fusion
  75.0 2.8 %collective-permute-done.1 = bf16[3,256]{1,0:T(4,128)(2,1)S(1)} collective-permute-done((bf16[3,256]{1,0:T(4,128)(2,1)S(1)}, bf16[3,256]{1,0:T(4,128)(2,1)S(1)}, u32[]{:S(2)}, u32[]{:S(2)}) %collective-permute-start.1) | collective-permute-done | bytes 1568 | tf_op jit(solution)/shard_map/ppermute | solution.py:58
  78.1 0.8 fusion.68
  79.0 0.7 multiply_convert_fusion.3
  80.3 0.9 copy.94
  81.6 2.0 while.13
  81.6 0.8 bitcast_dynamic-update-slice_fusion.2
  82.6 0.9 bitcast_dynamic-update-slice_fusion.2
  83.7 0.8 add_convert_fusion
  86.1 14.9 %all-reduce = bf16[128]{0:T(256)(128)(2,1)S(1)} all-reduce(bf16[128]{0:T(256)(128)(2,1)S(1)} %dynamic-update-slice), channel_id=2, replica_groups=mesh['x'=4,'z'=8,'y'=4,'c'=2] {'z'}, use_global_device_ids=true, to_apply=%add | all-reduce | flops 128 | bytes 512
  101.2 20.4 %all-gather.8.cloned.1.call-done = bf16[128,64,128]{2,1,0:T(8,128)(2,1)} async-done(((bf16[16,64,128]{2,1,0:T(8,128)(2,1)}), bf16[128,64,128]{2,1,0:T(8,128)(2,1)}) %all-gather.8.cloned.1.call-update) | async-done | bytes 2097168 | tf_op jit(solution)/shard_map/all_gather | solution.py:73
  121.6 2.8 %fusion.54 = bf16[1,16,64,128]{3,2,1,0:T(8,128)(2,1)} fusion(f32[16]{0:T(128)S(1)} %get-tuple-element.88, f32[16]{0:T(128)S(1)} %get-tuple-element.96, f32[16]{0:T(128)S(1)} %get-tuple-element.95, f32[16]{0:T(128)S(1)} %get-tuple-element.94, f32[16]{0:T(128)S(1)} %get-tuple-element.93, f32[16]{0:T(128)S(1)} %get-tuple-element.92, ...), kind=kLoop, calls=%fused_computation.87 | loop fusion | flops 3145728 | bytes 2359808 | tf_op jit(solution)/shard_map/convert_element_type | solution.py:73
  125.0 1.3 broadcast_in_dim.26
  126.3 7.6 %all-to-all-start = ((f32[32,1,1]{2,1,0:T(1,128)}), f32[32,1,1]{2,1,0:T(1,128)S(1)}, u32[]{:S(2)}, u32[]{:S(2)}) async-start(f32[32,1,1]{2,1,0:T(1,128)} %broadcast_in_dim.26), calls=%async_computation | async-start | bytes 32768 | tf_op jit(solution)/shard_map/all_to_all | solution.py:32
  133.9 8.0 %all-gather.2 = bf16[4,1,16]{2,1,0:T(2,128)(2,1)S(1)} all-gather(bf16[1,1,16]{2,1,0:T(2,128)(2,1)S(1)} %fusion.63), channel_id=1, replica_groups=mesh['x'=4,'z'=8,'y'=4,'c'=2] {'x'}, dimensions={0}, use_global_device_ids=true | all-gather | bytes 160 | tf_op jit(solution)/shard_map/all_gather | solution.py:73
  143.3 1.9 convolution_bitcast_fusion.1
  145.2 3.2 %all-gather.6.cloned.1.call-done = bf16[4,16,64,128]{3,2,1,0:T(8,128)(2,1)} async-done(((bf16[1,16,64,128]{3,2,1,0:T(8,128)(2,1)}), bf16[4,16,64,128]{3,2,1,0:T(8,128)(2,1)}) %all-gather.6.cloned.1.call-update) | async-done | bytes 1048592 | tf_op jit(solution)/shard_map/all_gather | solution.py:73
  148.5 3.1 %fusion.23 = f32[16,64,128]{2,1,0:T(8,128)S(1)} fusion(f32[16,64,128]{2,1,0:T(8,128)} %param.29, bf16[4,16,64,128]{3,2,1,0:T(8,128)(2,1)} %all-gather.6.cloned.1.call-done, f32[16]{0:T(128)S(1)} %get-tuple-element.88, f32[16]{0:T(128)S(1)} %get-tuple-element.96, f32[16]{0:T(128)S(1)} %get-tuple-element.95, f32[16]{0:T(128)S(1)} %get-tuple-element.94, ...), kind=kLoop, calls=%fused_computation.51 | loop fusion | flops 6422528 | bytes 4195149 | tf_op jit(solution)/shard_map/jit(_where)/select_n | solution.py:895
  151.6 3.5 %fusion.71 = (f32[2,128,16,64]{1,3,2,0:T(8,128)}, f32[2,128,16,64]{1,3,2,0:T(8,128)}) fusion(bf16[2,128,16,64]{1,3,2,0:T(8,128)(2,1)S(1)} %copy.94, f32[16]{0:T(128)S(1)} %copy-done.13, f32[2,128,16,64]{1,3,2,0:T(8,128)S(1)} %copy-done.6, f32[2,128,16]{1,2,0:T(8,128)S(1)} %copy.97, bf16[2,128,128]{2,1,0:T(8,128)(2,1)S(1)} %bitcast.192, ...), kind=kOutput, calls=%fused_computation.151 | convolution fusion | flops 404750336 | bytes 5324992 | tf_op jit(solution)/shard_map/cthn,chpn->cthp/dot_general | solution.py:900
  155.2 2.2 copy.103
  157.9 2.0 copy.100
  160.0 0.8 mul.506
  161.1 47.0 %out_projection.1 = bf16[32,4096]{1,0:T(8,128)(2,1)S(1)} custom-call(bf16[256,1024]{1,0:T(8,128)(2,1)S(1)} %multiply_convert_fusion.2.u_ref, f32[256,128]{1,0:T(8,128)S(1)} %copy.101.sq_ref, bf16[1024,128]{1,0:T(8,128)(2,1)S(1)} %copy-done.2), custom_call_target="tpu_custom_call" | custom-call | tf_op jit(solution)/shard_map/out_projection/pallas_call | solution.py:773
  208.1 0.7 copy.132
  (81 shorter events, 6.1 us)
Async XLA Ops:
  7.2 67.7 %copy-start.8 = (f32[4,1024]{1,0:T(4,128)S(1)}, f32[4,1024]{1,0:T(4,128)}, u32[]{:S(2)}) copy-start(f32[4,1024]{1,0:T(4,128)} %param.22) | copy-start | bytes 49156
  7.2 67.7 %copy-start.11 = (f32[4,1,2,128]{3,2,1,0:T(2,128)S(1)}, f32[4,1,2,128]{3,2,1,0:T(2,128)}, u32[]{:S(2)}) copy-start(f32[4,1,2,128]{3,2,1,0:T(2,128)} %param.23) | copy-start | bytes 12292
  7.2 70.6 %copy-start.12 = (bf16[3,1,2,128]{3,2,1,0:T(2,128)(2,1)S(1)}, bf16[3,1,2,128]{3,2,1,0:T(2,128)(2,1)}, u32[]{:S(2)}) copy-start(bf16[3,1,2,128]{3,2,1,0:T(2,128)(2,1)} %param.25) | copy-start | bytes 4612
  7.2 71.8 %copy-start.9 = (bf16[3,1024]{1,0:T(4,128)(2,1)S(1)}, bf16[3,1024]{1,0:T(4,128)(2,1)}, u32[]{:S(2)}) copy-start(bf16[3,1024]{1,0:T(4,128)(2,1)} %param.24) | copy-start | bytes 18436
  7.2 114.3 %all-gather.8.cloned.1.call-start = ((), (), s32[]{:S(2)}) async-start(), calls=%async_computation.2 | async-start | bytes 2359296 | tf_op jit(solution)/shard_map/all_gather | solution.py:73
  9.7 1.0 copy-start
  10.6 0.9 copy-start.1
  67.6 11.3 %collective-permute-start = (bf16[3,1024]{1,0:T(4,128)(2,1)S(1)}, bf16[3,1024]{1,0:T(4,128)(2,1)S(1)}, u32[]{:S(2)}, u32[]{:S(2)}) collective-permute-start(bf16[3,1024]{1,0:T(4,128)(2,1)S(1)} %slice.137), channel_id=1, source_target_pairs={{0,8},{8,16},{16,24},{24,32},{32,40},{40,48},{48,56},{56,64},{64,7... | collective-permute-start | bytes 18440 | tf_op jit(solution)/shard_map/ppermute | solution.py:58
  70.2 7.6 %collective-permute-start.1 = (bf16[3,256]{1,0:T(4,128)(2,1)S(1)}, bf16[3,256]{1,0:T(4,128)(2,1)S(1)}, u32[]{:S(2)}, u32[]{:S(2)}) collective-permute-start(bf16[3,256]{1,0:T(4,128)(2,1)S(1)} %slice.145), channel_id=1, source_target_pairs={{0,8},{8,16},{16,24},{24,32},{32,40},{40,48},{48,56},{56,64},{64,7... | collective-permute-start | bytes 4616 | tf_op jit(solution)/shard_map/ppermute | solution.py:58
  81.6 2.0 copy-start.4
  81.6 3.0 %copy-start.14 = (u32[256]{0:T(256)S(1)}, u32[256]{0:T(256)}, u32[]{:S(2)}) copy-start(u32[256]{0:T(256)} %constant.69) | copy-start | bytes 3076
  84.5 58.6 %copy-start.7 = (bf16[2,128,1,1,128]{4,3,1,0,2:T(2,128)(2,1)S(1)}, bf16[2,128,1,1,128]{4,3,1,0,2:T(2,128)(2,1)}, u32[]{:S(2)}) copy-start(bf16[2,128,1,1,128]{4,3,1,0,2:T(2,128)(2,1)} %get-tuple-element.73) | copy-start | bytes 196612
  84.5 63.9 %all-gather.6.cloned.1.call-start = ((), (), s32[]{:S(2)}) async-start(), calls=%async_computation.1 | async-start | bytes 1310720 | tf_op jit(solution)/shard_map/all_gather | solution.py:73
  126.3 16.2 %all-to-all-start = ((f32[32,1,1]{2,1,0:T(1,128)}), f32[32,1,1]{2,1,0:T(1,128)S(1)}, u32[]{:S(2)}, u32[]{:S(2)}) async-start(f32[32,1,1]{2,1,0:T(1,128)} %broadcast_in_dim.26), calls=%async_computation | async-start | bytes 32768 | tf_op jit(solution)/shard_map/all_to_all | solution.py:32
  142.1 6.3 %copy-start.3 = (bf16[128,64,128]{2,1,0:T(8,128)(2,1)S(1)}, bf16[128,64,128]{2,1,0:T(8,128)(2,1)}, u32[]{:S(2)}) copy-start(bf16[128,64,128]{2,1,0:T(8,128)(2,1)} %all-gather.8.cloned.1.call-done) | copy-start | bytes 6291460
  148.5 3.1 %copy-start.5 = (f32[2,16,64,128]{3,2,1,0:T(8,128)S(1)}, f32[2,16,64,128]{3,2,1,0:T(8,128)}, u32[]{:S(2)}) copy-start(f32[2,16,64,128]{3,2,1,0:T(8,128)} %get-tuple-element.37) | copy-start | bytes 3145732
  148.5 3.2 %copy-start.6 = (f32[2,128,16,64]{1,3,2,0:T(8,128)S(1)}, f32[2,128,16,64]{1,3,2,0:T(8,128)}, u32[]{:S(2)}) copy-start(f32[2,128,16,64]{1,3,2,0:T(8,128)} %convolution_bitcast_fusion.1) | copy-start | bytes 3145732
  148.5 3.2 %copy-start.13 = (f32[16]{0:T(128)S(1)}, f32[16]{0:T(128)}, u32[]{:S(2)}) copy-start(f32[16]{0:T(128)} %param.28) | copy-start | bytes 196
  159.9 1.0 copy-start.10
  160.0 1.1 copy-start.2
Sparse Core Ops, SparseCore 0:
  84.7 36.8 all-gather.7
  124.5 23.9 all-gather.5

commit v3 on v2

--- a/solution.py
+++ b/solution.py
@@ -1,10 +1,10 @@
 import jax
 import jax.numpy as jnp
 from jax import lax
+from jax.experimental import pallas as pl
+from jax.experimental.pallas import tpu as pltpu
 from jax.sharding import Mesh
 from jax.sharding import PartitionSpec as P
-from jax.experimental import pallas as pl
-from jax.experimental.pallas import tpu as pltpu
 
 HEADS = 128
 HEAD_DIM = 64
@@ -19,97 +19,6 @@
 
 epsilon = 1e-05
 quant_range = 448.0
-
-
-def in_order(parts, dim):
-    dims = list(parts.shape[1:])
-    dims[dim] *= parts.shape[0]
-    return jnp.moveaxis(parts, 0, dim).reshape(dims)
-
-
-def sent_to_all(shard, axis):
-    count = lax.axis_size(axis)
-    return lax.all_to_all(
-        jnp.broadcast_to(shard[None], (count, *shard.shape)), axis, 0, 0, tiled=True
-    )
-
-
-def gather_directly(shard, axis, dim):
-    return in_order(sent_to_all(shard, axis), dim)
-
-
-def over_copies(shard, axis):
-    everything = sent_to_all(shard, axis)
-    return jnp.max(everything, axis=0)
-
-
-def sent_together(arrays, axis, dim, along):
-    ends, at = ([], 0)
-    for a in arrays[:-1]:
-        at += a.shape[along]
-        ends.append(at)
-    both = jnp.concatenate(arrays, axis=along)
-    return tuple(jnp.split(lax.all_gather(both, axis, axis=dim, tiled=True), ends, axis=along))
-
-
-def from_behind(value, axis, steps):
-    count = lax.axis_size(axis)
-    first, last = (max(0, -steps), min(count, count - steps))
-    return lax.ppermute(value, axis, [(source, source + steps) for source in range(first, last)])
-
-
-def neutral_like(shard, identity):
-    return jax.tree.map(
-        lambda a, e: jnp.broadcast_to(jnp.asarray(e, a.dtype), a.shape), shard, identity
-    )
-
-
-def prefix_by_axis(shard, axes, combine, identity):
-    before = start = neutral_like(shard, identity)
-    total = shard
-    for axis in reversed(axes):
-        count, here = (lax.axis_size(axis), lax.axis_index(axis))
-        pieces = jax.tree.map(
-            lambda part, kind: lax.all_gather(part.astype(kind), axis),
-            total,
-            (jnp.bfloat16, jnp.bfloat16),
-        )
-        inside, total = (start, start)
-        for k in range(count):
-            passed = k < here
-            total = combine(
-                total, jax.tree.map(lambda part, own: part[k].astype(own.dtype), pieces, shard)
-            )
-            inside = jax.tree.map(lambda new, old: jnp.where(passed, new, old), total, inside)
-        before = combine(inside, before)
-    return before
-
-
-def taken_together(shard, axis):
-    return sent_to_all(shard, axis).sum(axis=0)
-
-
-def cut_along(shard, dim, count):
-    before, after = (shard.shape[:dim], shard.shape[dim + 1 :])
-    return jnp.moveaxis(shard.reshape(*before, count, -1, *after), dim, 0)
-
-
-def sent_and_summed(shard, axis, dim):
-    parts = cut_along(shard, dim, lax.axis_size(axis))
-    arrived = lax.all_to_all(parts, axis, split_axis=0, concat_axis=0, tiled=True)
-    return arrived.astype(jnp.float32).sum(axis=0)
-
-
-def depthwise(before, projected, conv_taps, length):
-    extended = jnp.concatenate([before, projected], axis=0)
-    summed = conv_taps[0] * extended[0:length]
-    for offset in range(1, KERNEL):
-        summed = summed + conv_taps[offset] * extended[offset : offset + length]
-    return jax.nn.silu(summed).astype(jnp.bfloat16)
-
-
-def combine(earlier, later):
-    return (earlier[0] * later[0], later[0][:, None, None] * earlier[1] + later[1])
 
 
 MESH_ID = pl.DeviceIdType.MESH
@@ -486,6 +395,342 @@
     )(jnp.reshape(prev_amax, (1,)), hidden_in, w_x, w_bc_dt)
 
 
+def scan_blocks(
+    x_ref,
+    bc_ref,
+    dt_ref,
+    top_ref,
+    conv_x_ref,
+    conv_bc_ref,
+    state_x_ref,
+    state_bc_ref,
+    par_ref,
+    init_ref,
+    gain_ref,
+    u_out,
+    sq_out,
+    max_out,
+    halo_x,
+    halo_bc,
+    ext,
+    x_act,
+    bc_act,
+    cum_s,
+    cum_t,
+    step_t,
+    expand,
+    added0,
+    device_state,
+    tiles,
+    arrived,
+    carried,
+    incoming,
+    init_t,
+    grown,
+    acc,
+    halo_send,
+    halo_recv,
+    tile_send,
+    tile_recv,
+    st_send,
+    st_recv,
+    back_send,
+    back_recv,
+):
+    x, z, y, c = (lax.axis_index(name) for name in ("x", "z", "y", "c"))
+    here = x * NZ + z
+    f32, bf16 = (jnp.float32, jnp.bfloat16)
+    count = NX * NZ
+
+    def at(rel):
+        dx, dz = (rel // NZ, rel % NZ)
+        return (lax.rem(x + dx, NX), lax.rem(z + dz, NZ), y, c)
+
+    def source(rel):
+        dx, dz = (rel // NZ, rel % NZ)
+        return (lax.rem(x + NX - dx, NX), lax.rem(z + NZ - dz, NZ))
+
+    def exact_dot(a, b):
+        return jnp.dot(a, b, precision=lax.Precision.HIGHEST, preferred_element_type=f32)
+
+    barrier = pltpu.get_barrier_semaphore()
+
+    def greet_one(rel, carry):
+        pl.semaphore_signal(barrier, inc=1, device_id=at(rel), device_id_type=MESH_ID)
+        return carry
+
+    lax.fori_loop(1, count, greet_one, 0)
+
+    lane = lax.broadcasted_iota(jnp.int32, (128, 1024), 1)
+    head = lax.broadcasted_iota(jnp.int32, (128, 1024), 0)
+    expand[...] = jnp.where((lane >= head * 64) & (lane < head * 64 + 64), 1.0, 0.0).astype(f32)
+    row_at = lax.broadcasted_iota(jnp.int32, (128, 128), 0)
+    col_at = lax.broadcasted_iota(jnp.int32, (128, 128), 1)
+    lower = row_at >= col_at
+    ones_lower = jnp.where(lower, 1.0, 0.0).astype(f32)
+    raw = dt_ref[...] + par_ref[0:1, :]
+    step = jnp.maximum(raw, 0.0) + jnp.log1p(jnp.exp(-jnp.abs(raw)))
+    lasts = []
+    shares = []
+    for b in range(2):
+        part = step[128 * b : 128 * b + 128]
+        cum = exact_dot(ones_lower, -part * par_ref[1:2, :])
+        cum_s[128 * b : 128 * b + 128, :] = cum
+        cum_t[b] = jnp.transpose(cum)[0:16]
+        step_t[b] = jnp.transpose(part)[0:16]
+        last = cum[127:128]
+        lasts.append(last)
+        shares.append(part * jnp.exp(last - cum))
+    top = jnp.max(top_ref[...], axis=0, keepdims=True)
+    first_row = lax.broadcasted_iota(jnp.int32, (8, 128), 0) == 0
+    tiles[here] = jnp.where(first_row, lasts[0] + lasts[1], top)
+
+    pl.semaphore_wait(barrier, count - 1)
+
+    next_z = lax.rem(z + 1, NZ)
+    next_x = lax.rem(x + (z + 1) // NZ, NX)
+    halo_copies = [
+        remote(ref.at[pl.ds(240, 16)], dst, halo_send.at[i], halo_recv.at[i], (next_x, next_z, y, c))
+        for i, (ref, dst) in enumerate(((x_ref, halo_x), (bc_ref, halo_bc)))
+    ]
+    for copy in halo_copies:
+        copy.start()
+
+    def tile_copy(rel):
+        return remote(
+            tiles.at[here], tiles.at[here], tile_send.at[rel], tile_recv.at[rel], at(rel)
+        )
+
+    def send_tile(rel, carry):
+        tile_copy(rel).start()
+        return carry
+
+    lax.fori_loop(1, count, send_tile, 0)
+
+    init_t[...] = jnp.transpose(
+        init_ref[pl.ds(pl.multiple_of(x * 256, 256), 256), :]
+    )
+
+    for b in range(2):
+        rows = slice(128 * b, 128 * b + 128)
+        ext[8 + 128 * b : 136 + 128 * b, 0:1024] = x_ref[rows, :].astype(f32)
+        ext[8 + 128 * b : 136 + 128 * b, 1024:1280] = bc_ref[rows, :].astype(f32)
+    for copy in halo_copies:
+        copy.wait_recv()
+    leading = here == 0
+    ext[5:8, 0:1024] = jnp.where(
+        leading, state_x_ref[...].astype(f32), halo_x[...].astype(f32)[13:16]
+    )
+    ext[5:8, 1024:1280] = jnp.where(
+        leading, state_bc_ref[...].astype(f32), halo_bc[...].astype(f32)[13:16]
+    )
+    for b in range(2):
+        for col in range(0, 1280, 256):
+            cols = slice(col, col + 256)
+            taps = conv_bc_ref[...] if col == 1024 else conv_x_ref[:, cols]
+            total = taps[0:1] * ext[5 + 128 * b : 133 + 128 * b, cols]
+            for k in range(1, KERNEL):
+                total = total + taps[k : k + 1] * ext[5 + k + 128 * b : 133 + k + 128 * b, cols]
+            value = (total / (1.0 + jnp.exp(-total))).astype(bf16)
+            if col == 1024:
+                bc_act[128 * b : 128 * b + 128, :] = value
+            else:
+                x_act[128 * b : 128 * b + 128, cols] = value
+
+    growth1 = exact_dot(jnp.exp(jnp.broadcast_to(lasts[1], (8, 128))), expand[...])[0:1]
+    for b in range(2):
+        rows = slice(128 * b, 128 * b + 128)
+        weighted = (x_act[rows, :].astype(f32) * exact_dot(shares[b], expand[...])).astype(bf16)
+        added = lax.dot_general(
+            bc_act[rows, 0:128], weighted, (((0,), (0,)), ((), ())), preferred_element_type=f32
+        )
+        if b == 0:
+            added0[...] = added
+        else:
+            device_state[...] = (growth1 * added0[...] + added).astype(bf16)
+
+    def slice_of(xs, zs):
+        return (
+            pl.ds(pl.multiple_of(zs * 16, 16), 16),
+            pl.ds(pl.multiple_of(xs * 256, 256), 256),
+        )
+
+    def state_copy(rel):
+        tx, tz, _, _ = at(rel)
+        return remote(
+            device_state.at[slice_of(tx, tz)],
+            arrived.at[here],
+            st_send.at[rel],
+            st_recv.at[rel],
+            at(rel),
+        )
+
+    growth0 = exact_dot(jnp.exp(jnp.broadcast_to(lasts[0], (8, 128))), expand[...])[0:1]
+    skips = exact_dot(jnp.broadcast_to(par_ref[2:3, :], (8, 128)), expand[...])[0:1]
+    grown[...] = jnp.concatenate([growth0, skips], axis=0)
+
+    def send_state(rel, carry):
+        state_copy(rel).start()
+        return carry
+
+    lax.fori_loop(1, count, send_state, 0)
+    arrived[here] = device_state[slice_of(x, z)]
+
+    half_lane = lax.broadcasted_iota(jnp.int32, (128, 128), 1) < 64
+
+    def block(b, carry):
+        rows = pl.ds(pl.multiple_of(b * 128, 128), 128)
+        meet = lax.dot_general(
+            bc_act[rows, 128:256],
+            bc_act[rows, 0:128],
+            (((1,), (1,)), ((), ())),
+            preferred_element_type=f32,
+        )
+        for pair in range(8):
+            cols = slice(128 * pair, 128 * pair + 128)
+            weights = []
+            for h in (2 * pair, 2 * pair + 1):
+                gap = cum_s[rows, h : h + 1] - cum_t[b, h : h + 1, :]
+                decay = jnp.exp(jnp.where(lower, gap, -1e30))
+                weights.append((meet * decay * step_t[b, h : h + 1, :]).astype(bf16))
+            values = x_act[rows, cols].astype(f32)
+            both = jnp.concatenate(
+                [jnp.where(half_lane, values, 0.0), jnp.where(half_lane, 0.0, values)], axis=0
+            ).astype(bf16)
+            part = jnp.dot(jnp.concatenate(weights, axis=1), both, preferred_element_type=f32)
+            acc[rows, cols] = part + grown[1:2, cols] * values
+        return carry
+
+    lax.fori_loop(0, 2, block, 0)
+
+    def tile_done(rel, carry):
+        sx, sz = source(rel)
+        ref = tiles.at[sx * NZ + sz]
+        remote(ref, ref, tile_send.at[rel], tile_recv.at[rel], at(rel)).wait_recv()
+        return carry
+
+    def state_done(rel, carry):
+        sx, sz = source(rel)
+        ref = arrived.at[sx * NZ + sz]
+        remote(ref, ref, st_send.at[rel], st_recv.at[rel], at(rel)).wait_recv()
+        return carry
+
+    lax.fori_loop(1, count, tile_done, 0)
+    everything = tiles[...]
+    logs = everything[:, 0, :]
+    max_out[...] = jnp.broadcast_to(
+        jnp.max(jnp.max(everything[:, 1, :], axis=0, keepdims=True), axis=1, keepdims=True), (8, 128)
+    )
+    decays = exact_dot(
+        jnp.exp(logs), expand[:, pl.ds(pl.multiple_of(x * 256, 256), 256)]
+    )
+    lax.fori_loop(1, count, state_done, 0)
+    state = init_t[pl.ds(pl.multiple_of(z * 16, 16), 16), :]
+    for s in range(count):
+        carried[s] = state.astype(bf16)
+        if s < count - 1:
+            state = decays[s : s + 1] * state + arrived[s].astype(f32)
+
+    def back_copy(rel):
+        tx, tz, _, _ = at(rel)
+        return remote(
+            carried.at[tx * NZ + tz],
+            incoming.at[slice_of(x, z)],
+            back_send.at[rel],
+            back_recv.at[rel],
+            at(rel),
+        )
+
+    def send_back(rel, carry):
+        back_copy(rel).start()
+        return carry
+
+    lax.fori_loop(1, count, send_back, 0)
+    incoming[slice_of(x, z)] = carried[here]
+
+    def back_done(rel, carry):
+        sx, sz = source(rel)
+        ref = incoming.at[slice_of(sx, sz)]
+        remote(ref, ref, back_send.at[rel], back_recv.at[rel], at(rel)).wait_recv()
+        return carry
+
+    lax.fori_loop(1, count, back_done, 0)
+
+    for b in range(2):
+        rows = slice(128 * b, 128 * b + 128)
+        entering = incoming[...]
+        if b == 1:
+            entering = (grown[0:1, :] * entering.astype(f32) + added0[...]).astype(bf16)
+        seen = jnp.dot(bc_act[rows, 128:256], entering, preferred_element_type=f32)
+        total = acc[rows, :] + exact_dot(jnp.exp(cum_s[rows, :]), expand[...]) * seen
+        u_out[rows, :] = (total * gain_ref[...]).astype(bf16)
+        squared = total * total
+        best = squared[:, 0:128]
+        for col in range(128, 1024, 128):
+            best = best + squared[:, col : col + 128]
+        sq_out[rows, :] = best
+
+    for copy in halo_copies:
+        copy.wait_send()
+
+    def sent(rel, carry):
+        tile_copy(rel).wait_send()
+        state_copy(rel).wait_send()
+        back_copy(rel).wait_send()
+        return carry
+
+    lax.fori_loop(1, count, sent, 0)
+
+
+def scan_all(x_whole, bc_whole, dt_raw, top, conv_x, conv_bc, state_x, state_bc, par, init, gain):
+    vmem = pl.BlockSpec(memory_space=pltpu.VMEM)
+    dma = pltpu.SemaphoreType.DMA
+    bf16, f32 = (jnp.bfloat16, jnp.float32)
+    count = NX * NZ
+    return pl.pallas_call(
+        scan_blocks,
+        name="scan_blocks",
+        out_shape=(
+            jax.ShapeDtypeStruct((256, 1024), bf16),
+            jax.ShapeDtypeStruct((256, 128), f32),
+            jax.ShapeDtypeStruct((8, 128), f32),
+        ),
+        in_specs=[vmem] * 11,
+        out_specs=(vmem, vmem, vmem),
+        scratch_shapes=[
+            pltpu.VMEM((16, 1024), bf16),
+            pltpu.VMEM((16, 256), bf16),
+            pltpu.VMEM((264, 1280), f32),
+            pltpu.VMEM((256, 1024), bf16),
+            pltpu.VMEM((256, 256), bf16),
+            pltpu.VMEM((256, 128), f32),
+            pltpu.VMEM((2, 16, 128), f32),
+            pltpu.VMEM((2, 16, 128), f32),
+            pltpu.VMEM((128, 1024), f32),
+            pltpu.VMEM((128, 1024), f32),
+            pltpu.VMEM((128, 1024), bf16),
+            pltpu.VMEM((count, 8, 128), f32),
+            pltpu.VMEM((count, 16, 256), bf16),
+            pltpu.VMEM((count, 16, 256), bf16),
+            pltpu.VMEM((128, 1024), bf16),
+            pltpu.VMEM((128, 256), f32),
+            pltpu.VMEM((2, 1024), f32),
+            pltpu.VMEM((256, 1024), f32),
+            dma((2,)),
+            dma((2,)),
+            dma((count,)),
+            dma((count,)),
+            dma((count,)),
+            dma((count,)),
+            dma((count,)),
+            dma((count,)),
+        ],
+        compiler_params=pltpu.CompilerParams(
+            collective_id=2, has_side_effects=True, vmem_limit_bytes=48 * 2**20
+        ),
+    )(x_whole, bc_whole, dt_raw, top, conv_x, conv_bc, state_x, state_bc, par, init, gain)
+
+
 GROUP_SLOTS = ((0, 4), (-1, 1), (-2, 2), (-3, 3))
 GROUP_ORDER = (1, 2, 3, 0)
 Y_NAMES = ("two_up", "two_down", "one_up_b", "one_down_a", "one_up_a", "one_down_b")
@@ -827,9 +1072,6 @@
     norm_gain,
     w_out,
 ):
-    margin = KERNEL - 1
-    leading = lax.axis_index(SEQ) == 0
-    row_count = hidden_in.shape[0] * 8
     bc_width = w_bc.shape[1] * w_bc.shape[2] * w_bc.shape[3]
     heads = w_dt.shape[1]
     w_bc_dt = jnp.concatenate(
@@ -840,72 +1082,23 @@
         ],
         axis=1,
     )
+    par = jnp.pad(jnp.stack([dt_bias, decay_rate, skip]), ((0, 5), (0, 128 - heads)))
     x_whole, bc_whole, dt_raw, top = project_in(prev_amax, hidden_in, w_x, w_bc_dt)
-    dt_raw = dt_raw[:, :heads]
-    abs_max = over_copies(jnp.max(top), SEQ)
-    state_bc = jnp.reshape(conv_state_bc, (margin, bc_width))
-    received = from_behind((x_whole[row_count - margin :], bc_whole[row_count - margin :]), SEQ, 1)
-    x_edge = jnp.where(leading, conv_state_x, received[0])
-    bc_edge = jnp.where(leading, state_bc, received[1])
-    x_act = depthwise(x_edge, x_whole, conv_x, row_count)
-    bc_act = depthwise(bc_edge, bc_whole, jnp.reshape(conv_bc, (KERNEL, bc_width)), row_count)
-    step_size = jax.nn.softplus(dt_raw + dt_bias)
-    heads_here = step_size.shape[1]
-    groups_here = w_bc.shape[1]
-    per_group = HEADS // GROUPS
-    blocks = row_count // SPAN
-    x_blocks = x_act.reshape(blocks, SPAN, heads_here, HEAD_DIM)
-    bc_blocks = bc_act.reshape(blocks, SPAN, groups_here, 2, STATE)
-    in_map = bc_blocks[:, :, :, 0]
-    out_map = bc_blocks[:, :, :, 1]
-    step_blocks = step_size.reshape(blocks, SPAN, heads_here)
-    cum_blocks = jnp.cumsum(-step_blocks * decay_rate, axis=1)
-    index_row = jnp.arange(SPAN, dtype=jnp.int32)
-    lower_mask = index_row[:, None] >= index_row[None, :]
-    intersection = jnp.einsum(
-        "ctgn,cugn->cgtu", out_map, in_map, preferred_element_type=jnp.float32
+    u, squares, largest = scan_all(
+        x_whole,
+        bc_whole,
+        dt_raw,
+        top,
+        conv_x,
+        jnp.reshape(conv_bc, (KERNEL, bc_width)),
+        conv_state_x,
+        jnp.reshape(conv_state_bc, (KERNEL - 1, bc_width)),
+        par,
+        jnp.reshape(init_state, (heads * HEAD_DIM, STATE)),
+        jnp.reshape(norm_gain, (1, -1)),
     )
-    intersection = jnp.repeat(intersection, per_group, axis=1)
-    cum_heads = jnp.transpose(cum_blocks, (0, 2, 1))
-    log_gap = cum_heads[:, :, :, None] - cum_heads[:, :, None, :]
-    decay = jnp.exp(jnp.where(lower_mask[None, None], log_gap, -1e30))
-    step_heads = jnp.transpose(step_blocks, (0, 2, 1))
-    weights = (intersection * decay * step_heads[:, :, None, :]).astype(jnp.bfloat16)
-    local_part = jnp.einsum(
-        "chtu,cuhp->cthp", weights, x_blocks, preferred_element_type=jnp.float32
-    )
-    last_cum = cum_blocks[:, SPAN - 1, :]
-    x_weighted = (
-        x_blocks.astype(jnp.float32)
-        * (step_blocks * jnp.exp(last_cum[:, None, :] - cum_blocks))[:, :, :, None]
-    ).astype(jnp.bfloat16)
-    in_heads = jnp.repeat(in_map, per_group, axis=2)
-    added = jnp.einsum("cuhp,cuhn->chpn", x_weighted, in_heads, preferred_element_type=jnp.float32)
-
-    def carry_on(carried, element):
-        block_decay, block_added = element
-        return (block_decay[:, None, None] * carried + block_added, carried)
-
-    empty_state = jnp.zeros((heads_here, HEAD_DIM, STATE), jnp.float32)
-    device_state, entering = lax.scan(carry_on, empty_state, (jnp.exp(last_cum), added))
-    device_decay = jnp.exp(jnp.sum(last_cum, axis=0))
-    seeded = device_state + jnp.where(leading, device_decay[:, None, None] * init_state, 0.0)
-    identity = (jnp.ones_like(device_decay), jnp.zeros_like(device_state))
-    scanned = prefix_by_axis((device_decay, seeded), SEQ, combine, identity)
-    incoming = jnp.where(leading, init_state, scanned[1])
-    prefix = jnp.exp(jnp.cumsum(last_cum, axis=0) - last_cum)
-    states_in = entering + prefix[:, :, None, None] * incoming[None]
-    out_heads = jnp.repeat(out_map, per_group, axis=2).astype(jnp.float32)
-    carried_part = (
-        jnp.einsum("cthn,chpn->cthp", out_heads, states_in, precision=lax.Precision.HIGHEST)
-        * jnp.exp(cum_blocks)[:, :, :, None]
-    )
-    ssm_out = local_part + carried_part + skip[None, None, :, None] * x_blocks.astype(jnp.float32)
-    ssm_out = ssm_out.reshape(row_count, heads_here * HEAD_DIM)
-    squares = jnp.sum((ssm_out * ssm_out).reshape(row_count, -1, 128), axis=1)
-    scaled_out = (ssm_out * norm_gain).astype(jnp.bfloat16)
-    layer_out = project_out(scaled_out, squares, w_out)
-    return (layer_out, abs_max)
+    layer_out = project_out(u, squares, w_out)
+    return (layer_out, largest[0, 0])
 
 
 def solution(mesh):

time: 216 us -> 145 us (0.67)
  Pallas kernels: 103 us -> 135 us
  waiting for transfers between devices: 26.8 us -> 0 us
  blocking collectives: 22.9 us -> 0 us
  between operations: 15.8 us -> 1.43 us
  starting transfers between devices: 13.2 us -> 0 us
  other arithmetic: 13 us -> 0.72 us
  local copies, waits for them, and re-layouts: 14.9 us -> 6.89 us
  matrix products: 6.02 us -> 0 us
    pallas_call x0 -> x1, Pallas kernels: none -> 34.6 us  [scan_all(): pl.pallas_call(scan_blocks, name='scan_blocks', out_shape=(jax.ShapeDtype...]
    all_gather x2 -> x0, waiting for transfers between devices: 23.6 us -> none  [prefix_by_axis(): lax.all_gather(part.astype(kind), axis)]
    unnamed x1 -> x0, blocking collectives: 14.9 us -> none
    all_gather x1 -> x0, blocking collectives: 8.01 us -> none  [prefix_by_axis(): lax.all_gather(part.astype(kind), axis)]
    all_to_all x1 -> x0, starting transfers between devices: 7.58 us -> none  [sent_to_all(): lax.all_to_all(jnp.broadcast_to(shard[None], (count, *shard.shape)), axis...]
    dot_general x4 -> x0, matrix products: 6.02 us -> none  [the longest x1 3.53 us: local(): jnp.einsum('cthn,chpn->cthp', out_heads, states_in, precision=lax.Precisi...]
    ppermute x2 -> x0, starting transfers between devices: 5.5 us -> none  [from_behind(): lax.ppermute(value, axis, [(source, source + steps) for source in range(f...]
    convert_element_type x7 -> x0, other arithmetic: 4.67 us -> none  [the longest x2 3.62 us: prefix_by_axis(): part.astype(kind)]
  transfers between devices with their start and end apart: 5 -> 0, of which waited for: 4 -> 0; matrix products, arithmetic and copies ran while one was open for 4% -> 0% of each run, Pallas kernels for 0% -> 0%
where the time goes in v3:
time: 145 us; the launch traced here: 144 us
  Pallas kernels  135 us (93%)
  local copies, waits for them, and re-layouts  6.89 us (5%)
    pallas_call x1, Pallas kernels, project_in(): pl.pallas_call(in_projection, name='in_projection', out_shape=(jax.ShapeD...  56 us
    pallas_call x1, Pallas kernels, project_out(): pl.pallas_call(out_projection, name='out_projection', out_shape=jax.Shape...  44.6 us
    pallas_call x1, Pallas kernels, scan_all(): pl.pallas_call(scan_blocks, name='scan_blocks', out_shape=(jax.ShapeDtype...  34.6 us
    unnamed x19, local copies, waits for them, and re-layouts  6.29 us

profile of v3, /device:TPU:2, one launch (start us, length us, event | category | flops | bytes accessed | tf_op | source)
XLA Modules:
  0.0 144.2 jit_solution(5565687021143927261)
XLA Ops:
  0.6 0.0 copy-start
  1.4 0.1 pad.10.clone
  1.4 0.7 copy.26
  2.1 0.7 copy.25
  2.8 0.7 select_maximum_fusion.par_ref
  3.5 0.8 copy.17
  4.3 0.9 copy.24
  5.2 0.0 copy-start.1
  5.2 0.9 copy-done.1
  6.1 0.0 copy-start.2
  6.1 0.9 copy-done.2
  7.1 0.0 copy-start.4
  7.1 0.0 copy-start.5
  7.1 56.0 %in_projection.1 = (bf16[256,1024]{1,0:T(8,128)(2,1)S(1)}, bf16[256,256]{1,0:T(8,128)(2,1)S(1)}, f32[256,128]{1,0:T(8,128)S(1)}, f32[8,128]{1,0:T(8,128)S(1)}) custom-call(f32[1]{0:T(128)} %bitcast.22.amax_ref, bf16[32,4096]{1,0:T(8,128)(2,1)S(1)} %copy-done.1, bf16[128,1024]{1,0:T(8,128)(2,1)S(1)} %copy-done.2, bf16[128,384]{1,0:T(8,128)(2,1)S(1)} %maximum_maximum_fusion.wbd_ref), custom_call_target="tpu_custom_call" | custom-call | tf_op jit(solution)/shard_map/in_projection/pallas_call | solution.py:361
  63.1 0.0 copy-start.6
  63.1 0.0 copy-done
  63.1 0.0 copy-done.4
  63.2 0.0 copy-done.5
  63.2 0.6 copy-done.6
  63.8 0.0 copy-start.3
  63.8 34.6 %scan_blocks.1 = (bf16[256,1024]{1,0:T(8,128)(2,1)S(1)}, f32[256,128]{1,0:T(8,128)S(1)}, f32[8,128]{1,0:T(8,128)S(1)}) custom-call(bf16[256,1024]{1,0:T(8,128)(2,1)S(1)} %get-tuple-element.9.x_ref, bf16[256,256]{1,0:T(8,128)(2,1)S(1)} %get-tuple-element.10.bc_ref, f32[256,128]{1,0:T(8,128)S(1)} %get-tuple-element.11.dt_ref, ...), custom_call_target="tpu_custom_call" | custom-call | tf_op jit(solution)/shard_map/scan_blocks/pallas_call | solution.py:690
  98.4 0.5 slice.3
  98.9 0.0 copy-done.3
  98.9 44.6 %out_projection.1 = bf16[32,4096]{1,0:T(8,128)(2,1)S(1)} custom-call(bf16[256,1024]{1,0:T(8,128)(2,1)S(1)} %get-tuple-element.13.u_ref, f32[256,128]{1,0:T(8,128)S(1)} %get-tuple-element.14.sq_ref, bf16[1024,128]{1,0:T(8,128)(2,1)S(1)} %copy-done.3), custom_call_target="tpu_custom_call" | custom-call | tf_op jit(solution)/shard_map/out_projection/pallas_call | solution.py:1018
  143.5 0.7 copy.29
  (2 shorter events, 0.0 us)
Async XLA Ops:
  0.6 62.5 %copy-start = (f32[16,64,128]{2,1,0:T(8,128)S(1)}, f32[16,64,128]{2,1,0:T(8,128)}, u32[]{:S(2)}) copy-start(f32[16,64,128]{2,1,0:T(8,128)} %param.27) | copy-start | bytes 1572868
  5.2 1.0 copy-start.1
  6.1 0.9 copy-start.2
  7.1 56.0 %copy-start.4 = (f32[4,1024]{1,0:T(4,128)S(1)}, f32[4,1024]{1,0:T(4,128)}, u32[]{:S(2)}) copy-start(f32[4,1024]{1,0:T(4,128)} %conv_x_ref.1) | copy-start | bytes 49156
  7.1 56.1 %copy-start.5 = (bf16[3,1024]{1,0:T(4,128)(2,1)S(1)}, bf16[3,1024]{1,0:T(4,128)(2,1)}, u32[]{:S(2)}) copy-start(bf16[3,1024]{1,0:T(4,128)(2,1)} %state_x_ref.1) | copy-start | bytes 18436
  63.1 0.7 copy-start.6
  63.8 35.1 %copy-start.3 = (bf16[1024,128]{1,0:T(8,128)(2,1)S(1)}, bf16[1024,128]{1,0:T(8,128)(2,1)}, u32[]{:S(2)}) copy-start(bf16[1024,128]{1,0:T(8,128)(2,1)} %w_ref.1) | copy-start | bytes 786436

commit v4 on v1

v4 whole, which is shorter than its diff:
```python
import jax
import jax.numpy as jnp
from jax import lax
from jax.experimental import pallas as pl
from jax.experimental.pallas import tpu as pltpu
from jax.sharding import Mesh
from jax.sharding import PartitionSpec as P

HEADS = 128
HEAD_DIM = 64
STATE = 128
GROUPS = 8
KERNEL = 4
SPAN = 128
SEQ = ("x", "z")
TENSOR = ("y", "c")
SEQ_TENSOR = SEQ + TENSOR


epsilon = 1e-05
quant_range = 448.0


MESH_ID = pl.DeviceIdType.MESH
NX, NZ, NY, NC = (4, 8, 4, 2)
COUNT = NX * NZ
CHUNKS = (384, 256, 256, 256, 256)
STARTS = (0, 384, 640, 896, 1152)
WIDE = 1408
X_ROWS = 1024
TWO_UP, TWO_DOWN, ONE_UP_B, ONE_DOWN_A, ONE_UP_A, ONE_DOWN_B = range(6)
SLOTS = (0, 4, -1, 1, -2, 2, -3, 3)
(S_HX, S_HY, S_SIB, S_RS, S_HALO, S_TILE, S_ST, S_BACK, S_U, S_O, S_SQ, S_C, S_Y, S_F) = range(14)
S_Z = 14
OTHERS = tuple((dy, dc) for dy in range(NY) for dc in range(NC) if (dy, dc) != (0, 0))


def scratch():
    bf16, f32 = (jnp.bfloat16, jnp.float32)
    v, dma = (pltpu.VMEM, pltpu.SemaphoreType.DMA)
    return [
        v((4, NC, NY, 32, X_ROWS), bf16),
        v((4, 256, X_ROWS), bf16),
        v((X_ROWS, CHUNKS[0]), bf16),
        v((X_ROWS, CHUNKS[1]), bf16),
        v((X_ROWS, CHUNKS[2]), bf16),
        v((X_ROWS, CHUNKS[3]), bf16),
        v((X_ROWS, CHUNKS[4]), bf16),
        v((3, 256, WIDE), bf16),
        v((256, WIDE), bf16),
        v((512, WIDE), bf16),
        v((256, WIDE), f32),
        v((128, WIDE), f32),
        v((128, WIDE), f32),
        v((8, 128), f32),
        v((16, 1280), bf16),
        v((16, 1280), bf16),
        v((264, 1280), f32),
        v((256, 1024), bf16),
        v((256, 256), bf16),
        v((256, 128), f32),
        v((256, 128), f32),
        v((256, 128), f32),
        v((2, 16, 128), f32),
        v((2, 16, 128), f32),
        v((2, 128, 128), f32),
        v((8, 128), f32),
        v((4, 8, 256), f32),
        v((128, 1024), f32),
        v((128, 1024), f32),
        v((128, 1024), bf16),
        v((COUNT, 8, 128), f32),
        v((COUNT, 16, 256), bf16),
        v((COUNT, 16, 256), bf16),
        v((128, 1024), bf16),
        v((128, 256), f32),
        v((256, 1024), f32),
        v((256, 128), f32),
        v((4, 256, 1024), bf16),
        v((1024, 1024), bf16),
        v((4, NC, NY, 32, 1024), bf16),
        v((4, NY, 32, 1024), bf16),
        v((4, NY, 32, 1024), bf16),
        v((4, 32, 1024), bf16),
        v((4, 2, 32, 1024), bf16),
        v((4, 32, 1024), f32),
        v((4, 16, 1024), f32),
        v((4, 16, 1024), f32),
        v((4, 32, 1024), bf16),
        v((4, 32, 1024), bf16),
        v((7, 32, 128), f32),
        dma((8,)),
        dma((19,)),
        dma((4,)),
        dma((4,)),
        dma((4,)),
        dma((2, 5, 3)),
        dma((5,)),
        dma((5, 2)),
        dma((5,)),
        dma((5,)),
        dma((1,)),
        dma((1,)),
        dma((4,)),
        dma((4, 2)),
        dma((3,)),
        dma((2, 4, 3)),
        dma((1,)),
        dma((1,)),
        dma((4,)),
        dma((4, 2)),
        dma((4,)),
        dma((1,)),
    ]


def remote(src, dst, send_sem, recv_sem, where):
    return pltpu.make_async_remote_copy(
        src_ref=src,
        dst_ref=dst,
        send_sem=send_sem,
        recv_sem=recv_sem,
        device_id=where,
        device_id_type=MESH_ID,
    )


def layer(
    amax_ref,
    hid_ref,
    wx_ref,
    wbd_ref,
    conv_x_ref,
    conv_bc_ref,
    state_x_ref,
    state_bc_ref,
    par_ref,
    init_ref,
    gain_ref,
    w_ref,
    out_ref,
    max_out,
    rows,
    quant,
    w0,
    w1,
    w2,
    w3,
    w4,
    stage,
    r1,
    r2,
    own,
    plus,
    minus,
    top,
    tail_out,
    tail_in,
    ext,
    x_act,
    bc_act,
    dt_s,
    cum_s,
    share_s,
    cum_t,
    step_t,
    meet,
    rates,
    grown,
    expand,
    added0,
    device_state,
    tiles,
    arrived,
    carried,
    incoming,
    init_t,
    acc,
    sq,
    tokens,
    weights,
    partial,
    from_core,
    ystage,
    ry1,
    ry2,
    yown,
    yup,
    ydown,
    fstage,
    landed,
    squares,
    local_sem,
    sent_sem,
    hx_recv,
    hy_recv,
    sib_recv,
    z_recv,
    z_last,
    rs_recv,
    rs_last,
    halo_recv,
    tile_recv,
    st_recv,
    back_recv,
    u_recv,
    u_last,
    o_recv,
    o_last,
    sq_recv,
    c_recv,
    y_recv,
    y_last,
    f_recv,
):
    x, z, y, c = (lax.axis_index(name) for name in ("x", "z", "y", "c"))
    here = x * NZ + z
    f32, bf16 = (jnp.float32, jnp.bfloat16)
    wbuf = (w0, w1, w2, w3, w4)

    def at(dx=0, dz=0, dy=0, dc=0):
        return (
            lax.rem(x + dx + NX, NX),
            lax.rem(z + dz + NZ, NZ),
            lax.rem(y + dy + NY, NY),
            lax.rem(c + dc, NC),
        )

    def at_rel(rel):
        return (lax.rem(x + rel // NZ, NX), lax.rem(z + rel % NZ, NZ), y, c)

    def x_of(r):
        return lax.rem(x + r + NX, NX)

    def y_of(dy):
        return lax.rem(y + dy + NY, NY)

    def t_index(dy, dc):
        return y_of(dy) * NC + lax.rem(c + dc, NC)

    def exact_dot(a, b):
        return jnp.dot(a, b, precision=lax.Precision.HIGHEST, preferred_element_type=f32)

    def go(copy):
        copy.start()

    def take(ref, sem):
        remote(ref, ref, sent_sem.at[0], sem, at(dz=1)).wait_recv()

    def drain(ref, index):
        remote(ref, ref, sent_sem.at[index], hx_recv.at[0], at(dz=1)).wait_send()

    def z_rows(dz, low=0, count=128):
        block = lax.rem(z + dz + NZ, NZ)
        return pl.ds(pl.multiple_of(block * 128 + low, count), count)

    def z_cols(slot):
        return pl.ds(128 * SLOTS.index(slot), 128)

    local = []
    for j in range(5):
        src = wbd_ref if j == 0 else wx_ref.at[:, pl.ds(256 * (j - 1), 256)]
        local.append(pltpu.make_async_copy(src, wbuf[j].at[z_rows(0)], local_sem.at[j]))
    local.append(
        pltpu.make_async_copy(
            hid_ref.at[:, pl.ds(pl.multiple_of(x * X_ROWS, X_ROWS), X_ROWS)],
            rows.at[x, c, y],
            local_sem.at[5],
        )
    )
    local.append(pltpu.make_async_copy(w_ref, weights.at[:, z_cols(0)], local_sem.at[6]))
    for copy in local:
        copy.start()

    barrier = pltpu.get_barrier_semaphore()

    def greet(rel, carry):
        pl.semaphore_signal(barrier, inc=1, device_id=at_rel(rel), device_id_type=MESH_ID)
        return carry

    lax.fori_loop(1, COUNT, greet, 0)
    for dy, dc in OTHERS:
        pl.semaphore_signal(barrier, inc=1, device_id=at(dy=dy, dc=dc), device_id_type=MESH_ID)

    lane = lax.broadcasted_iota(jnp.int32, (128, 1024), 1)
    head = lax.broadcasted_iota(jnp.int32, (128, 1024), 0)
    expand[...] = jnp.where((lane >= head * 64) & (lane < head * 64 + 64), 1.0, 0.0).astype(f32)
    row_at = lax.broadcasted_iota(jnp.int32, (128, 128), 0)
    col_at = lax.broadcasted_iota(jnp.int32, (128, 128), 1)
    lower = row_at >= col_at
    ones_lower = jnp.where(lower, 1.0, 0.0).astype(f32)
    init_t[...] = jnp.transpose(init_ref[pl.ds(pl.multiple_of(x * 256, 256), 256), :])
    for copy in local:
        copy.wait()
    pl.semaphore_wait(barrier, COUNT - 1 + len(OTHERS))

    def z_copy(j, k, d):
        sign = 1 if d == 0 else -1
        piece = z_rows(-sign * k) if k < 3 else z_rows(-sign * k, 64 * d, 64)
        ref = wbuf[j].at[piece]
        sem = z_recv.at[d, j, k] if k < 3 else z_last.at[j]
        return remote(ref, ref, sent_sem.at[S_Z + j], sem, at(dz=sign))

    def z_step(j, k):
        for d in range(2):
            if k > 0:
                sign = 1 if d == 0 else -1
                take(wbuf[j].at[z_rows(-sign * k)], z_recv.at[d, j, k - 1])
            go(z_copy(j, k, d))

    def hx_copy(r):
        dest = lax.rem(x + NX - r, NX)
        src = hid_ref.at[:, pl.ds(pl.multiple_of(dest * X_ROWS, X_ROWS), X_ROWS)]
        return remote(src, rows.at[x, c, y], sent_sem.at[S_HX], hx_recv.at[r], at(dx=-r))

    def hy_first(r):
        ref = rows.at[x_of(r), c, y]
        if r > 0:
            take(ref, hx_recv.at[r])
        for dy in (1, 3, 2):
            go(remote(ref, ref, sent_sem.at[S_HY], hy_recv.at[r], at(dy=dy)))

    def hy_pass(r):
        take(rows.at[x_of(r), c, pl.ds(0, 3)], hy_recv.at[r])
        ref = rows.at[x_of(r), c]
        go(remote(ref, ref, sent_sem.at[S_SIB], sib_recv.at[r], at(dc=1)))

    largest = jnp.zeros((8, 128), jnp.float32)
    amax = jnp.full((8, 128), amax_ref[0], jnp.float32)
    factor = (quant_range / amax)[0:1, 0:1]
    in_scale = (amax / quant_range)[0:1, 0:1]
    top[...] = largest

    def quantized(r):
        where = x_of(r)
        take(rows.at[where, lax.rem(c + 1, NC)], sib_recv.at[r])

        def tile(i, carry):
            core, place = (i // NY, lax.rem(i, NY))
            part = pl.ds(pl.multiple_of((place * NC + core) * 32, 32), 32)
            value = rows[where, core, place].astype(jnp.float32)
            quant[where, part, :] = jnp.clip(
                value * factor, -quant_range, quant_range
            ).astype(jnp.bfloat16)
            most = jnp.max(jnp.abs(value).reshape(4, 8, 1024), axis=0)
            best = most[:, 0:128]
            for lane in range(128, 1024, 128):
                best = jnp.maximum(best, most[:, lane : lane + 128])
            top[...] = jnp.maximum(top[...], best)
            return carry

        lax.fori_loop(0, 8, tile, 0)

    def ext_cols(j):
        return slice(1024, 1280) if j == 0 else slice(256 * (j - 1), 256 * j)

    def halo_copy(j):
        next_z = lax.rem(z + 1, NZ)
        next_x = lax.rem(x + (z + 1) // NZ, NX)
        where = (next_x, next_z, y, c)
        part = pl.ds(ext_cols(j).start, 256)
        return remote(
            tail_out.at[:, part], tail_in.at[:, part], sent_sem.at[S_HALO], halo_recv.at[j], where
        )

    def cols(j):
        return pl.ds(STARTS[j], CHUNKS[j])

    def rs_copy(j, name):
        slot, low, dst, dst_low, sign = {
            TWO_UP: (0, 0, r1, 0, 1),
            TWO_DOWN: (0, 128, r1, 128, -1),
            ONE_UP_B: (1, 128, r2, 128, 1),
            ONE_DOWN_A: (2, 0, r2, 256, -1),
            ONE_UP_A: (1, 0, r2, 0, 1),
            ONE_DOWN_B: (2, 128, r2, 384, -1),
        }[name]
        return remote(
            stage.at[slot, pl.ds(low, 128), cols(j)],
            dst.at[pl.ds(dst_low, 128), cols(j)],
            sent_sem.at[S_RS],
            rs_recv.at[j, name] if name < 2 else rs_last.at[j],
            at(dx=sign),
        )

    def product(j, r):
        return jnp.dot(quant[x_of(r)], wbuf[j][...], preferred_element_type=jnp.float32)

    def rs_multiply(j):
        take(wbuf[j].at[pl.ds(0, 128)], z_last.at[j])
        stage[0, :, cols(j)] = product(j, 2).astype(jnp.bfloat16)
        value = product(j, 1)
        plus[:, cols(j)] = value[0:128]
        stage[1, 128:256, cols(j)] = value[128:256].astype(jnp.bfloat16)
        go(rs_copy(j, TWO_UP))
        go(rs_copy(j, TWO_DOWN))
        value = product(j, 3)
        minus[:, cols(j)] = value[128:256]
        stage[2, 0:128, cols(j)] = value[0:128].astype(jnp.bfloat16)
        go(rs_copy(j, ONE_UP_B))
        own[:, cols(j)] = product(j, 0)
        go(rs_copy(j, ONE_DOWN_A))

    def rs_add(j):
        rs_copy(j, TWO_UP).wait_recv()
        stage[1, 0:128, cols(j)] = (
            plus[:, cols(j)] + r1[0:128, cols(j)].astype(jnp.float32)
        ).astype(jnp.bfloat16)
        rs_copy(j, TWO_DOWN).wait_recv()
        stage[2, 128:256, cols(j)] = (
            minus[:, cols(j)] + r1[128:256, cols(j)].astype(jnp.float32)
        ).astype(jnp.bfloat16)
        go(rs_copy(j, ONE_UP_A))
        go(rs_copy(j, ONE_DOWN_B))

    def rs_final(j):
        take(r2.at[:, cols(j)], rs_last.at[j])
        total = (
            own[:, cols(j)]
            + r2[0:256, cols(j)].astype(jnp.float32)
            + r2[256:512, cols(j)].astype(jnp.float32)
        ) * in_scale
        value = total[:, 0:256].astype(bf16)
        ext[8:264, ext_cols(j)] = value.astype(f32)
        tail_out[:, ext_cols(j)] = value[240:256]
        if j == 0:
            dt_s[...] = total[:, 256:384]
        go(halo_copy(j))

    def tile_copy(rel):
        return remote(
            tiles.at[here], tiles.at[here], sent_sem.at[S_TILE], tile_recv.at[0], at_rel(rel)
        )

    def steps():
        raw = dt_s[...] + par_ref[0:1, :]
        step = jnp.maximum(raw, 0.0) + jnp.log1p(jnp.exp(-jnp.abs(raw)))
        lasts = []
        for b in range(2):
            part = step[128 * b : 128 * b + 128]
            cum = exact_dot(ones_lower, -part * par_ref[1:2, :])
            cum_s[128 * b : 128 * b + 128, :] = cum
            cum_t[b] = jnp.transpose(cum)[0:16]
            step_t[b] = jnp.transpose(part)[0:16]
            last = cum[127:128]
            lasts.append(last)
            share_s[128 * b : 128 * b + 128, :] = part * jnp.exp(last - cum)
        most = jnp.max(top[...], axis=0, keepdims=True)
        row8 = lax.broadcasted_iota(jnp.int32, (8, 128), 0)
        tiles[here] = jnp.where(row8 == 0, lasts[0] + lasts[1], most)
        rates[...] = jnp.where(
            row8 == 0, jnp.exp(lasts[0]), jnp.where(row8 == 1, jnp.exp(lasts[1]), par_ref[2:3, :])
        )

        def send_tile(rel, carry):
            tile_copy(rel).start()
            return carry

        lax.fori_loop(1, COUNT, send_tile, 0)

    def convolve(j):
        halo_copy(j).wait_recv()
        part = ext_cols(j)
        before = state_bc_ref[...] if j == 0 else state_x_ref[:, part]
        ext[5:8, part] = jnp.where(
            here == 0, before.astype(f32), tail_in[:, part].astype(f32)[13:16]
        )
        taps = conv_bc_ref[...] if j == 0 else conv_x_ref[:, part]
        for b in range(2):
            total = taps[0:1] * ext[5 + 128 * b : 133 + 128 * b, part]
            for k in range(1, KERNEL):
                total = total + taps[k : k + 1] * ext[5 + k + 128 * b : 133 + k + 128 * b, part]
            value = (total / (1.0 + jnp.exp(-total))).astype(bf16)
            if j == 0:
                bc_act[128 * b : 128 * b + 128, :] = value
                meet[b] = lax.dot_general(
                    value[:, 128:256],
                    value[:, 0:128],
                    (((1,), (1,)), ((), ())),
                    preferred_element_type=f32,
                )
            else:
                x_act[128 * b : 128 * b + 128, part] = value

    def slice_of(xs, zs):
        return (
            pl.ds(pl.multiple_of(zs * 16, 16), 16),
            pl.ds(pl.multiple_of(xs * 256, 256), 256),
        )

    def state_copy(g, dz):
        tz = lax.rem(z + dz, NZ)
        return remote(
            device_state.at[pl.ds(pl.multiple_of(tz * 16, 16), 16), pl.ds(256 * g, 256)],
            arrived.at[here],
            sent_sem.at[S_ST],
            st_recv.at[0],
            (g, tz, y, c),
        )

    def add_states(g):
        part = slice(256 * g, 256 * g + 256)
        spread = expand[:, part]
        rate = exact_dot(rates[...], spread)
        grown[g] = rate
        for b in range(2):
            rows_b = slice(128 * b, 128 * b + 128)
            weighted = (
                x_act[rows_b, part].astype(f32) * exact_dot(share_s[rows_b, :], spread)
            ).astype(bf16)
            added = lax.dot_general(
                bc_act[rows_b, 0:128], weighted, (((0,), (0,)), ((), ())), preferred_element_type=f32
            )
            if b == 0:
                added0[:, part] = added
            else:
                device_state[:, part] = (rate[1:2] * added0[:, part] + added).astype(bf16)

        @pl.when(x == g)
        def _():
            arrived[here] = device_state[pl.ds(pl.multiple_of(z * 16, 16), 16), part]

        @pl.when(x != g)
        def _():
            state_copy(g, 0).start()

        for dz in range(1, NZ):
            state_copy(g, dz).start()

    half_lane = lax.broadcasted_iota(jnp.int32, (128, 128), 1) < 64

    def inside(g):
        def block(b, carry):
            rows_b = pl.ds(pl.multiple_of(b * 128, 128), 128)
            for pair in (2 * g, 2 * g + 1):
                part = slice(128 * pair, 128 * pair + 128)
                both_weights = []
                for h in (2 * pair, 2 * pair + 1):
                    gap = cum_s[rows_b, h : h + 1] - cum_t[b, h : h + 1, :]
                    decay = jnp.exp(jnp.where(lower, gap, -1e30))
                    both_weights.append((meet[b] * decay * step_t[b, h : h + 1, :]).astype(bf16))
                values = x_act[rows_b, part].astype(f32)
                both = jnp.concatenate(
                    [jnp.where(half_lane, values, 0.0), jnp.where(half_lane, 0.0, values)], axis=0
                ).astype(bf16)
                result = jnp.dot(
                    jnp.concatenate(both_weights, axis=1), both, preferred_element_type=f32
                )
                low = 128 * (pair - 2 * g)
                acc[rows_b, part] = result + grown[g, 2:3, low : low + 128] * values
            return carry

        lax.fori_loop(0, 2, block, 0)

    def back_copy(rel):
        tx, tz, _, _ = at_rel(rel)
        return remote(
            carried.at[tx * NZ + tz],
            incoming.at[slice_of(x, z)],
            sent_sem.at[S_BACK],
            back_recv.at[x],
            at_rel(rel),
        )

    def chain(g):
        @pl.when(x == g)
        def _():
            take(tiles.at[pl.ds(0, COUNT - 1)], tile_recv.at[0])
            everything = tiles[...]
            best = jnp.max(everything[:, 1, :], axis=0, keepdims=True)
            max_out[...] = jnp.broadcast_to(jnp.max(best, axis=1, keepdims=True), (8, 128))
            decays = exact_dot(jnp.exp(everything[:, 0, :]), expand[:, 256 * g : 256 * g + 256])

            take(arrived.at[pl.ds(0, COUNT - 1)], st_recv.at[0])
            state = init_t[pl.ds(pl.multiple_of(z * 16, 16), 16), :]
            for n in range(COUNT):
                carried[n] = state.astype(bf16)
                if n < COUNT - 1:
                    state = decays[n : n + 1] * state + arrived[n].astype(f32)

            def send_back(rel, carry):
                back_copy(rel).start()
                return carry

            lax.fori_loop(1, COUNT, send_back, 0)
            incoming[slice_of(x, z)] = carried[here]

    def u_copy(g, b, kind, origin, where):
        ref = tokens.at[x_of(origin), pl.ds(128 * b, 128), pl.ds(256 * g, 256)]
        sem = u_recv.at[g, b] if kind == b else u_last.at[kind]
        return remote(ref, ref, sent_sem.at[S_U], sem, where)

    def finish(g):
        part = slice(256 * g, 256 * g + 256)

        @pl.when(x != g)
        def _():
            take(incoming.at[:, part], back_recv.at[g])

        @pl.when(x == g)
        def _():
            take(incoming.at[pl.ds(0, 112), part], back_recv.at[g])

        for b in range(2):
            rows_b = slice(128 * b, 128 * b + 128)
            entering = incoming[:, part]
            if b == 1:
                entering = (grown[g, 0:1, :] * entering.astype(f32) + added0[:, part]).astype(bf16)
            seen = jnp.dot(bc_act[rows_b, 128:256], entering, preferred_element_type=f32)
            total = acc[rows_b, part] + exact_dot(jnp.exp(cum_s[rows_b, :]), expand[:, part]) * seen
            tokens[x, rows_b, part] = (total * gain_ref[:, part]).astype(bf16)
            squared = total * total
            squared = squared[:, 0:128] + squared[:, 128:256]
            sq[rows_b, :] = squared if g == 0 else sq[rows_b, :] + squared
        go(u_copy(g, 0, 0, 0, at(dx=1)))
        go(u_copy(g, 1, 1, 0, at(dx=-1)))
        go(u_copy(g, 1, 0, 0, at(dx=1)))
        go(u_copy(g, 0, 1, 0, at(dx=-1)))

    def u_relay(g):
        take(tokens.at[0, pl.ds(0, 128), pl.ds(0, 256)], u_recv.at[g, 0])
        go(u_copy(g, 0, 2, -1, at(dx=1)))
        take(tokens.at[0, pl.ds(0, 128), pl.ds(0, 256)], u_recv.at[g, 1])
        go(u_copy(g, 1, 2, 1, at(dx=-1)))

    def o_copy(j, k, d):
        sign = 1 if d == 0 else -1
        rows_j = pl.ds(256 * j, 256)
        arrives = 4 if k == 3 else -sign * (k + 1)
        return remote(
            weights.at[rows_j, z_cols(-sign * k)],
            weights.at[rows_j, z_cols(arrives)],
            sent_sem.at[S_O],
            o_recv.at[d, j, k] if k < 3 else o_last.at[0],
            at(dz=sign),
        )

    def o_wave(k, pieces=(0, 1, 2, 3)):
        for j in pieces:
            for d in range(2):
                if k > 0:
                    o_copy(j, k - 1, d).wait_recv()
                if k < 3 or j // 2 == d:
                    go(o_copy(j, k, d))

    def sq_copy(n):
        dy, dc = OTHERS[n]
        there = pl.ds(pl.multiple_of(t_index(dy, dc) * 32, 32), 32)
        return remote(sq.at[there], squares.at[n], sent_sem.at[S_SQ], sq_recv.at[0], at(dy=dy, dc=dc))

    def multiply(r):
        slot = x_of(r)

        def one(n, carry):
            part = pl.ds(pl.multiple_of(n * 256, 256), 256)
            value = jnp.dot(
                tokens[slot], weights[:, part], preferred_element_type=jnp.float32
            ).astype(jnp.bfloat16)
            value = value.reshape(NY, NC, 32, 256)
            for core in range(NC):
                partial[r, core, :, :, part] = value[:, core]
            return carry

        lax.fori_loop(0, 4, one, 0)
        go(c_copy(r))

    def c_copy(r):
        other = lax.rem(c + 1, NC)
        return remote(
            partial.at[r, other], from_core.at[r], sent_sem.at[S_C], c_recv.at[r], at(dc=1)
        )

    def y_copy(r, name):
        slot, low, dst, sign = {
            TWO_UP: (2, 0, ry1.at[r], 1),
            TWO_DOWN: (2, 16, ry1.at[r], -1),
            ONE_UP_B: (1, 16, ry2.at[r, 0], 1),
            ONE_DOWN_A: (3, 0, ry2.at[r, 1], -1),
            ONE_UP_A: (1, 0, ry2.at[r, 0], 1),
            ONE_DOWN_B: (3, 16, ry2.at[r, 1], -1),
        }[name]
        return remote(
            ystage.at[r, slot, pl.ds(low, 16)],
            dst.at[pl.ds(low, 16)],
            sent_sem.at[S_Y],
            y_recv.at[r, name] if name < 2 else y_last.at[r],
            at(dy=sign),
        )

    def both_cores(r, dy):
        where = y_of(dy)
        return partial[r, c, where].astype(jnp.float32) + from_core[r, where].astype(jnp.float32)

    def y_first(r):
        take(from_core.at[r], c_recv.at[r])
        ystage[r, 2] = both_cores(r, 2).astype(jnp.bfloat16)
        value = both_cores(r, 1)
        yup[r] = value[0:16]
        ystage[r, 1, 16:32] = value[16:32].astype(jnp.bfloat16)
        go(y_copy(r, TWO_UP))
        go(y_copy(r, TWO_DOWN))
        value = both_cores(r, 3)
        ydown[r] = value[16:32]
        ystage[r, 3, 0:16] = value[0:16].astype(jnp.bfloat16)
        go(y_copy(r, ONE_UP_B))
        yown[r] = both_cores(r, 0)
        go(y_copy(r, ONE_DOWN_A))

    def y_add(r):
        y_copy(r, TWO_UP).wait_recv()
        ystage[r, 1, 0:16] = (yup[r] + ry1[r, 0:16].astype(jnp.float32)).astype(jnp.bfloat16)
        y_copy(r, TWO_DOWN).wait_recv()
        ystage[r, 3, 16:32] = (ydown[r] + ry1[r, 16:32].astype(jnp.float32)).astype(jnp.bfloat16)
        go(y_copy(r, ONE_UP_A))
        go(y_copy(r, ONE_DOWN_B))

    def y_final(r):
        take(ry2.at[r], y_last.at[r])
        value = (
            yown[r] + ry2[r, 0].astype(jnp.float32) + ry2[r, 1].astype(jnp.float32)
        ).astype(jnp.bfloat16)
        if r == 0:
            landed[x] = value
        else:
            fstage[r] = value
            go(remote(fstage.at[r], landed.at[x], sent_sem.at[S_F], f_recv.at[0], at(dx=r)))

    for r in (1, 3, 2):
        go(hx_copy(r))
    hy_first(0)
    z_step(0, 0)
    z_step(1, 0)
    hy_first(1)
    hy_first(3)
    z_step(0, 1)
    hy_first(2)
    z_step(1, 1)
    hy_pass(0)
    z_step(0, 2)
    z_step(1, 2)
    z_step(2, 0)
    hy_pass(1)
    z_step(0, 3)
    z_step(3, 0)
    hy_pass(3)
    z_step(1, 3)
    z_step(2, 1)
    z_step(4, 0)
    hy_pass(2)
    for r in (0, 1, 3, 2):
        quantized(r)
    rs_multiply(0)
    z_step(3, 1)
    rs_multiply(1)
    z_step(2, 2)
    z_step(3, 2)
    rs_add(0)
    z_step(4, 1)
    z_step(2, 3)
    z_step(3, 3)
    rs_add(1)
    z_step(4, 2)
    rs_multiply(2)
    rs_final(0)
    rs_multiply(3)
    z_step(4, 3)
    o_wave(0)
    steps()
    rs_add(2)
    rs_multiply(4)
    rs_final(1)
    convolve(0)
    rs_add(3)
    convolve(1)
    add_states(0)
    o_wave(1, (0, 1))
    rs_add(4)
    rs_final(2)
    convolve(2)
    add_states(1)
    o_wave(1, (2, 3))
    inside(0)
    rs_final(3)
    chain(0)
    convolve(3)
    add_states(2)
    inside(1)
    o_wave(2)
    rs_final(4)
    chain(1)
    convolve(4)
    add_states(3)
    inside(2)
    inside(3)
    finish(0)
    chain(2)
    o_wave(3)
    finish(1)
    u_relay(0)
    chain(3)
    finish(2)
    u_relay(1)
    finish(3)
    for n in range(7):
        go(sq_copy(n))
    take(weights.at[:, pl.ds(0, 128)], o_last.at[0])
    u_relay(2)
    multiply(0)
    u_relay(3)
    y_first(0)
    take(tokens.at[0, pl.ds(0, 128)], u_last.at[0])
    multiply(3)
    take(tokens.at[0, pl.ds(0, 128)], u_last.at[1])
    y_add(0)
    multiply(1)
    y_first(3)
    take(tokens.at[0], u_last.at[2])
    multiply(2)
    y_first(1)
    y_add(3)
    y_final(0)
    y_first(2)
    y_add(1)
    y_final(3)
    y_add(2)
    y_final(1)

    take(squares, sq_recv.at[0])
    index = t_index(0, 0)
    total = sq[pl.ds(pl.multiple_of(index * 32, 32), 32), :]
    for n in range(7):
        total = total + squares[n]
    mean_sq = jnp.sum(total, axis=1, keepdims=True) / (HEADS * HEAD_DIM)
    scale = lax.rsqrt(mean_sq + epsilon)

    y_final(2)
    drain(rows.at[0, 0, pl.ds(0, 3)], S_HX)
    drain(rows.at[pl.ds(0, 3), 0], S_HY)
    drain(rows.at[:, 0], S_SIB)
    for j in range(5):
        drain(wbuf[j].at[pl.ds(0, 896)], S_Z + j)
    drain(stage, S_RS)
    drain(tail_out, S_HALO)
    drain(tiles.at[pl.ds(0, COUNT - 1)], S_TILE)
    drain(arrived.at[pl.ds(0, COUNT - 1)], S_ST)
    drain(arrived.at[pl.ds(0, COUNT - 1)], S_BACK)
    drain(tokens.at[pl.ds(0, 3)], S_U)
    drain(weights.at[pl.ds(0, 896)], S_O)
    drain(squares, S_SQ)
    drain(from_core, S_C)
    drain(ystage.at[:, pl.ds(0, 3)], S_Y)
    drain(fstage.at[pl.ds(0, 3)], S_F)
    take(landed.at[pl.ds(0, 3)], f_recv.at[0])
    for block in range(NX):
        for n, slot in enumerate(SLOTS):
            place = lax.rem(z + slot + NZ, NZ)
            part = pl.ds(pl.multiple_of(1024 * block + place * 128, 128), 128)
            value = landed[block, :, 128 * n : 128 * n + 128].astype(f32)
            out_ref[:, part] = (value * scale).astype(bf16)


def run_layer(*arrays):
    vmem = pl.BlockSpec(memory_space=pltpu.VMEM)
    any_place = pl.BlockSpec(memory_space=pl.ANY)
    return pl.pallas_call(
        layer,
        name="layer",
        out_shape=(
            jax.ShapeDtypeStruct((32, 4096), jnp.bfloat16),
            jax.ShapeDtypeStruct((8, 128), jnp.float32),
        ),
        in_specs=[pl.BlockSpec(memory_space=pltpu.SMEM)]
        + [any_place] * 3
        + [vmem] * 7
        + [any_place],
        out_specs=(vmem, vmem),
        scratch_shapes=scratch(),
        compiler_params=pltpu.CompilerParams(
            collective_id=0, has_side_effects=True, vmem_limit_bytes=60 * 2**20
        ),
    )(*arrays)


def local(
    hidden_in,
    prev_amax,
    w_x,
    w_bc,
    w_dt,
    conv_x,
    conv_bc,
    conv_state_x,
    conv_state_bc,
    dt_bias,
    decay_rate,
    skip,
    init_state,
    norm_gain,
    w_out,
):
    bc_width = w_bc.shape[1] * w_bc.shape[2] * w_bc.shape[3]
    heads = w_dt.shape[1]
    w_bc_dt = jnp.concatenate(
        [
            jnp.reshape(w_bc, (w_bc.shape[0], bc_width)),
            w_dt,
            jnp.zeros((w_dt.shape[0], 128 - heads), w_dt.dtype),
        ],
        axis=1,
    )
    layer_out, largest = run_layer(
        jnp.reshape(prev_amax, (1,)),
        hidden_in,
        w_x,
        w_bc_dt,
        conv_x,
        jnp.reshape(conv_bc, (KERNEL, bc_width)),
        conv_state_x,
        jnp.reshape(conv_state_bc, (KERNEL - 1, bc_width)),
        jnp.pad(jnp.stack([dt_bias, decay_rate, skip]), ((0, 5), (0, 128 - heads))),
        jnp.reshape(init_state, (heads * HEAD_DIM, STATE)),
        jnp.reshape(norm_gain, (1, -1)),
        w_out,
    )
    return (layer_out, largest[0, 0])


def solution(mesh):
    finer = Mesh(mesh.devices.reshape(NX, NZ, NY, NC), SEQ_TENSOR)
    return jax.shard_map(
        local,
        mesh=finer,
        in_specs=(
            P(SEQ_TENSOR, None),
            P(),
            P(SEQ, TENSOR),
            P(SEQ, TENSOR, None, None),
            P(SEQ, TENSOR),
            P(None, TENSOR),
            P(None, TENSOR, None, None),
            P(None, TENSOR),
            P(None, TENSOR, None, None),
            P(TENSOR),
            P(TENSOR),
            P(TENSOR),
            P(TENSOR, None, None),
            P(TENSOR),
            P(TENSOR, SEQ),
        ),
        out_specs=(P(SEQ_TENSOR, None), P()),
        check_vma=False,
    )
```

time: 303 us -> 132 us (0.44)
  waiting for transfers between devices: 145 us -> 0 us
  Pallas kernels: 56 us -> 121 us
  starting transfers between devices: 24.6 us -> 0 us
  blocking collectives: 22.8 us -> 0 us
  between operations: 15.4 us -> 1.34 us
  other arithmetic: 14 us -> 1.95 us
  matrix products: 11.9 us -> 0 us
  local copies, waits for them, and re-layouts: 11 us -> 6.31 us
    all_gather x3 -> x0, waiting for transfers between devices: 111 us -> none  [the longest x1 78 us: local(): lax.all_gather(w_out, SEQ, axis=1, tiled=True)]
    pallas_call x1, Pallas kernels: 56 us -> 121 us  [run_layer(): pl.pallas_call(layer, name='layer', out_shape=(jax.ShapeDtypeStruct((32,...]
    all_to_all x3 -> x0, waiting for transfers between devices: 30.4 us -> none  [the longest x1 26.5 us: sent_and_summed(): lax.all_to_all(parts, axis, split_axis=0, concat_axis=0, tiled=True)]
    all_to_all x3 -> x0, starting transfers between devices: 19 us -> none  [the longest x2 14.7 us: sent_to_all(): lax.all_to_all(jnp.broadcast_to(shard[None], (count, *shard.shape)), axis...]
    unnamed x1 -> x0, blocking collectives: 14.9 us -> none
    dot_general x5 -> x0, matrix products: 11.9 us -> none  [the longest x1 7.24 us: local(): jnp.dot(normed, lax.all_gather(w_out, SEQ, axis=1, tiled=True), preferred...]
    all_gather x1 -> x0, blocking collectives: 7.88 us -> none  [prefix_by_axis(): lax.all_gather(part.astype(kind), axis)]
    ppermute x2 -> x0, starting transfers between devices: 5.5 us -> none  [from_behind(): lax.ppermute(value, axis, [(source, source + steps) for source in range(f...]
  transfers between devices with their start and end apart: 8 -> 0, of which waited for: 6 -> 0; matrix products, arithmetic and copies ran while one was open for 8% -> 0% of each run, Pallas kernels for 0% -> 0%
where the time goes in v4:
time: 132 us; the launch traced here: 131 us
  Pallas kernels  121 us (92%)
  local copies, waits for them, and re-layouts  6.31 us (5%)
  other arithmetic  1.95 us (1%)
  between operations  1.34 us (1%)
    pallas_call x1, Pallas kernels, run_layer(): pl.pallas_call(layer, name='layer', out_shape=(jax.ShapeDtypeStruct((32,...  121 us
    unnamed x7, local copies, waits for them, and re-layouts  5.04 us

profile of v4, /device:TPU:2, one launch (start us, length us, event | category | flops | bytes accessed | tf_op | source)
XLA Modules:
  0.0 130.9 jit_solution(16169637738501133712)
XLA Ops:
  0.6 0.0 copy-start
  1.3 0.1 pad.10.clone
  1.4 1.3 copy.26
  2.7 1.3 copy.25
  4.0 1.3 select_maximum_fusion.par_ref
  5.2 0.8 copy.17
  6.0 0.0 copy-done
  6.1 0.7 maximum_maximum_fusion.wbd_ref
  6.7 121.3 %layer.1 = (bf16[32,4096]{1,0:T(8,128)(2,1)}, f32[8,128]{1,0:T(8,128)}) custom-call(f32[1]{0:T(128)} %bitcast.22.amax_ref, bf16[32,4096]{1,0:T(8,128)(2,1)} %hid_ref.1, bf16[128,1024]{1,0:T(8,128)(2,1)} %wx_ref.1, bf16[128,384]{1,0:T(8,128)(2,1)} %maximum_maximum_fusion.wbd_ref, f32[4,1024]{1,0:T(4,128)} %conv_x_ref.1, f32[4,256]{1,0:T(4,128)} %bitcast.26, ...), custom_call_target="tpu_custom_call" | custom-call | tf_op jit(solution)/shard_map/layer/pallas_call | solution.py:865
  128.0 1.2 slice.3
  129.2 1.7 %copy.29 = bf16[32,4096]{1,0:T(8,128)(2,1)} copy(bf16[32,4096]{1,0:T(8,128)(2,1)} %get-tuple-element.8) | data formatting | bytes 524288
  (2 shorter events, 0.0 us)
Async XLA Ops:
  0.6 5.4 %copy-start = (bf16[128,1,2,128]{3,2,1,0:T(2,128)(2,1)S(1)}, bf16[128,1,2,128]{3,2,1,0:T(2,128)(2,1)}, u32[]{:S(2)}) copy-start(bf16[128,1,2,128]{3,2,1,0:T(2,128)(2,1)} %param.18) | copy-start | bytes 196612

commit v5 on v4

--- a/solution.py
+++ b/solution.py
@@ -39,6 +39,7 @@
     bf16, f32 = (jnp.bfloat16, jnp.float32)
     v, dma = (pltpu.VMEM, pltpu.SemaphoreType.DMA)
     return [
+        v((8, 128), f32),
         v((4, NC, NY, 32, X_ROWS), bf16),
         v((4, 256, X_ROWS), bf16),
         v((X_ROWS, CHUNKS[0]), bf16),
@@ -129,17 +130,21 @@
     amax_ref,
     hid_ref,
     wx_ref,
-    wbd_ref,
+    wbc_ref,
+    wdt_ref,
     conv_x_ref,
     conv_bc_ref,
     state_x_ref,
     state_bc_ref,
-    par_ref,
+    bias_ref,
+    decay_ref,
+    skip_ref,
     init_ref,
     gain_ref,
     w_ref,
     out_ref,
     max_out,
+    par_ref,
     rows,
     quant,
     w0,
@@ -257,10 +262,22 @@
     def z_cols(slot):
         return pl.ds(128 * SLOTS.index(slot), 128)
 
-    local = []
-    for j in range(5):
-        src = wbd_ref if j == 0 else wx_ref.at[:, pl.ds(256 * (j - 1), 256)]
-        local.append(pltpu.make_async_copy(src, wbuf[j].at[z_rows(0)], local_sem.at[j]))
+    barrier = pltpu.get_barrier_semaphore()
+
+    def greet(rel, carry):
+        pl.semaphore_signal(barrier, inc=1, device_id=at_rel(rel), device_id_type=MESH_ID)
+        return carry
+
+    lax.fori_loop(1, COUNT, greet, 0)
+    for dy, dc in OTHERS:
+        pl.semaphore_signal(barrier, inc=1, device_id=at(dy=dy, dc=dc), device_id_type=MESH_ID)
+
+    local = [
+        pltpu.make_async_copy(
+            wx_ref.at[:, pl.ds(256 * (j - 1), 256)], wbuf[j].at[z_rows(0)], local_sem.at[j]
+        )
+        for j in range(1, 5)
+    ]
     local.append(
         pltpu.make_async_copy(
             hid_ref.at[:, pl.ds(pl.multiple_of(x * X_ROWS, X_ROWS), X_ROWS)],
@@ -272,15 +289,19 @@
     for copy in local:
         copy.start()
 
-    barrier = pltpu.get_barrier_semaphore()
-
-    def greet(rel, carry):
-        pl.semaphore_signal(barrier, inc=1, device_id=at_rel(rel), device_id_type=MESH_ID)
-        return carry
-
-    lax.fori_loop(1, COUNT, greet, 0)
-    for dy, dc in OTHERS:
-        pl.semaphore_signal(barrier, inc=1, device_id=at(dy=dy, dc=dc), device_id_type=MESH_ID)
+    maps = wbc_ref[...].astype(f32)
+    wbuf[0][z_rows(0), 0:128] = maps[:, 0, 0, :].astype(bf16)
+    wbuf[0][z_rows(0), 128:256] = maps[:, 0, 1, :].astype(bf16)
+    for_steps = jnp.concatenate([wdt_ref[...].astype(f32), jnp.zeros((112, 128), f32)], axis=0)
+    wbuf[0][z_rows(0), 256:384] = jnp.transpose(for_steps).astype(bf16)
+    par_ref[...] = jnp.zeros((8, 128), f32)
+    par_ref[0:1, 0:16] = bias_ref[...]
+    par_ref[1:2, 0:16] = decay_ref[...]
+    par_ref[2:3, 0:16] = skip_ref[...]
+
+    def side_by_side(ref, k):
+        pair = ref[k, 0].astype(f32)
+        return jnp.concatenate([pair[0:1], pair[1:2]], axis=1)
 
     lane = lax.broadcasted_iota(jnp.int32, (128, 1024), 1)
     head = lax.broadcasted_iota(jnp.int32, (128, 1024), 0)
@@ -461,11 +482,14 @@
     def convolve(j):
         halo_copy(j).wait_recv()
         part = ext_cols(j)
-        before = state_bc_ref[...] if j == 0 else state_x_ref[:, part]
+        if j == 0:
+            before = jnp.concatenate([side_by_side(state_bc_ref, k) for k in range(3)], axis=0)
+            taps = jnp.concatenate([side_by_side(conv_bc_ref, k) for k in range(KERNEL)], axis=0)
+        else:
+            before, taps = (state_x_ref[:, part].astype(f32), conv_x_ref[:, part])
         ext[5:8, part] = jnp.where(
-            here == 0, before.astype(f32), tail_in[:, part].astype(f32)[13:16]
-        )
-        taps = conv_bc_ref[...] if j == 0 else conv_x_ref[:, part]
+            here == 0, before, tail_in[:, part].astype(f32)[13:16]
+        )
         for b in range(2):
             total = taps[0:1] * ext[5 + 128 * b : 133 + 128 * b, part]
             for k in range(1, KERNEL):
@@ -568,7 +592,7 @@
             take(tiles.at[pl.ds(0, COUNT - 1)], tile_recv.at[0])
             everything = tiles[...]
             best = jnp.max(everything[:, 1, :], axis=0, keepdims=True)
-            max_out[...] = jnp.broadcast_to(jnp.max(best, axis=1, keepdims=True), (8, 128))
+            max_out[...] = jnp.max(best, axis=1, keepdims=True)
             decays = exact_dot(jnp.exp(everything[:, 0, :]), expand[:, 256 * g : 256 * g + 256])
 
             take(arrived.at[pl.ds(0, COUNT - 1)], st_recv.at[0])
@@ -737,18 +761,20 @@
     z_step(1, 1)
     hy_pass(0)
     z_step(0, 2)
+    hy_pass(1)
     z_step(1, 2)
     z_step(2, 0)
-    hy_pass(1)
+    hy_pass(3)
     z_step(0, 3)
     z_step(3, 0)
-    hy_pass(3)
+    hy_pass(2)
     z_step(1, 3)
     z_step(2, 1)
     z_step(4, 0)
-    hy_pass(2)
-    for r in (0, 1, 3, 2):
-        quantized(r)
+    quantized(0)
+    quantized(1)
+    quantized(3)
+    quantized(2)
     rs_multiply(0)
     z_step(3, 1)
     rs_multiply(1)
@@ -761,68 +787,70 @@
     rs_add(1)
     z_step(4, 2)
     rs_multiply(2)
-    rs_final(0)
     rs_multiply(3)
     z_step(4, 3)
     o_wave(0)
-    steps()
+    rs_final(0)
     rs_add(2)
     rs_multiply(4)
+    steps()
     rs_final(1)
+    rs_add(3)
     convolve(0)
-    rs_add(3)
+    rs_final(2)
+    rs_add(4)
     convolve(1)
     add_states(0)
     o_wave(1, (0, 1))
-    rs_add(4)
-    rs_final(2)
+    rs_final(3)
     convolve(2)
     add_states(1)
     o_wave(1, (2, 3))
-    inside(0)
-    rs_final(3)
-    chain(0)
+    rs_final(4)
     convolve(3)
     add_states(2)
-    inside(1)
-    o_wave(2)
-    rs_final(4)
-    chain(1)
+    inside(0)
     convolve(4)
     add_states(3)
+    o_wave(2, (0, 1))
+    chain(0)
+    inside(1)
+    chain(1)
     inside(2)
     inside(3)
+    o_wave(2, (2, 3))
+    chain(2)
+    chain(3)
+    o_wave(3, (0, 1))
     finish(0)
-    chain(2)
-    o_wave(3)
     finish(1)
     u_relay(0)
-    chain(3)
+    o_wave(3, (2, 3))
     finish(2)
     u_relay(1)
     finish(3)
+    u_relay(2)
     for n in range(7):
         go(sq_copy(n))
     take(weights.at[:, pl.ds(0, 128)], o_last.at[0])
-    u_relay(2)
     multiply(0)
+    y_first(0)
     u_relay(3)
-    y_first(0)
     take(tokens.at[0, pl.ds(0, 128)], u_last.at[0])
     multiply(3)
+    y_add(0)
     take(tokens.at[0, pl.ds(0, 128)], u_last.at[1])
-    y_add(0)
     multiply(1)
     y_first(3)
     take(tokens.at[0], u_last.at[2])
     multiply(2)
     y_first(1)
     y_add(3)
-    y_final(0)
     y_first(2)
     y_add(1)
+    y_final(0)
+    y_add(2)
     y_final(3)
-    y_add(2)
     y_final(1)
 
     take(squares, sq_recv.at[0])
@@ -867,11 +895,11 @@
         name="layer",
         out_shape=(
             jax.ShapeDtypeStruct((32, 4096), jnp.bfloat16),
-            jax.ShapeDtypeStruct((8, 128), jnp.float32),
+            jax.ShapeDtypeStruct((1, 1), jnp.float32),
         ),
         in_specs=[pl.BlockSpec(memory_space=pltpu.SMEM)]
-        + [any_place] * 3
-        + [vmem] * 7
+        + [any_place] * 2
+        + [vmem] * 11
         + [any_place],
         out_specs=(vmem, vmem),
         scratch_shapes=scratch(),
@@ -898,26 +926,20 @@
     norm_gain,
     w_out,
 ):
-    bc_width = w_bc.shape[1] * w_bc.shape[2] * w_bc.shape[3]
     heads = w_dt.shape[1]
-    w_bc_dt = jnp.concatenate(
-        [
-            jnp.reshape(w_bc, (w_bc.shape[0], bc_width)),
-            w_dt,
-            jnp.zeros((w_dt.shape[0], 128 - heads), w_dt.dtype),
-        ],
-        axis=1,
-    )
     layer_out, largest = run_layer(
         jnp.reshape(prev_amax, (1,)),
         hidden_in,
         w_x,
-        w_bc_dt,
+        w_bc,
+        jnp.transpose(w_dt),
         conv_x,
-        jnp.reshape(conv_bc, (KERNEL, bc_width)),
+        conv_bc,
         conv_state_x,
-        jnp.reshape(conv_state_bc, (KERNEL - 1, bc_width)),
-        jnp.pad(jnp.stack([dt_bias, decay_rate, skip]), ((0, 5), (0, 128 - heads))),
+        conv_state_bc,
+        jnp.reshape(dt_bias, (1, heads)),
+        jnp.reshape(decay_rate, (1, heads)),
+        jnp.reshape(skip, (1, heads)),
         jnp.reshape(init_state, (heads * HEAD_DIM, STATE)),
         jnp.reshape(norm_gain, (1, -1)),
         w_out,

time: 132 us -> 117 us (0.89)
  Pallas kernels: 121 us -> 112 us
  local copies, waits for them, and re-layouts: 6.31 us -> 1.67 us
  other arithmetic: 1.95 us -> 0 us
  between operations: 1.34 us -> 3.06 us
    pallas_call x1, Pallas kernels: 121 us -> 112 us  [run_layer(): pl.pallas_call(layer, name='layer', out_shape=(jax.ShapeDtypeStruct((32,...]
    unnamed x7 -> x1, local copies, waits for them, and re-layouts: 5.04 us -> 1.67 us
where the time goes in v5:
time: 117 us
  Pallas kernels  112 us (96%)
  between operations  3.06 us (3%)
  local copies, waits for them, and re-layouts  1.67 us (1%)
    pallas_call x1, Pallas kernels, run_layer(): pl.pallas_call(layer, name='layer', out_shape=(jax.ShapeDtypeStruct((32,...  112 us

profile of v5, /device:TPU:2, one launch (start us, length us, event | category | flops | bytes accessed | tf_op | source)
XLA Modules:
  0.0 117.1 jit_solution(14377968962689116928)
XLA Ops:
  1.3 112.4 %layer.1 = (bf16[32,4096]{1,0:T(8,128)(2,1)}, f32[1,1]{1,0:T(1,128)}) custom-call(f32[1]{0:T(128)} %bitcast.8.amax_ref, bf16[32,4096]{1,0:T(8,128)(2,1)} %hid_ref.1, bf16[128,1024]{1,0:T(8,128)(2,1)} %wx_ref.1, bf16[128,1,2,128]{3,2,1,0:T(2,128)(2,1)} %wbc_ref.1, bf16[16,128]{1,0:T(8,128)(2,1)} %bitcast.10, f32[4,1024]{1,0:T(4,128)} %conv_x_ref.1, ...), custom_call_target="tpu_custom_call" | custom-call | tf_op jit(solution)/shard_map/layer/pallas_call | solution.py:893
  113.7 1.7 %copy.20 = bf16[32,4096]{1,0:T(8,128)(2,1)} copy(bf16[32,4096]{1,0:T(8,128)(2,1)} %get-tuple-element.8) | data formatting | bytes 524288

commit v6 on v5

--- a/solution.py
+++ b/solution.py
@@ -264,11 +264,9 @@
 
     barrier = pltpu.get_barrier_semaphore()
 
-    def greet(rel, carry):
-        pl.semaphore_signal(barrier, inc=1, device_id=at_rel(rel), device_id_type=MESH_ID)
-        return carry
-
-    lax.fori_loop(1, COUNT, greet, 0)
+    beside = (at(dx=1), at(dx=-1), at(dx=2), at(dz=1), at(dz=-1))
+    for peer in beside:
+        pl.semaphore_signal(barrier, inc=1, device_id=peer, device_id_type=MESH_ID)
     for dy, dc in OTHERS:
         pl.semaphore_signal(barrier, inc=1, device_id=at(dy=dy, dc=dc), device_id_type=MESH_ID)
 
@@ -313,7 +311,7 @@
     init_t[...] = jnp.transpose(init_ref[pl.ds(pl.multiple_of(x * 256, 256), 256), :])
     for copy in local:
         copy.wait()
-    pl.semaphore_wait(barrier, COUNT - 1 + len(OTHERS))
+    pl.semaphore_wait(barrier, len(beside) + len(OTHERS))
 
     def z_copy(j, k, d):
         sign = 1 if d == 0 else -1
@@ -796,36 +794,34 @@
     steps()
     rs_final(1)
     rs_add(3)
+    o_wave(1, (0, 1))
     convolve(0)
     rs_final(2)
     rs_add(4)
     convolve(1)
     add_states(0)
-    o_wave(1, (0, 1))
     rs_final(3)
     convolve(2)
     add_states(1)
-    o_wave(1, (2, 3))
     rs_final(4)
     convolve(3)
     add_states(2)
     inside(0)
     convolve(4)
     add_states(3)
-    o_wave(2, (0, 1))
+    o_wave(1, (2, 3))
     chain(0)
     inside(1)
     chain(1)
     inside(2)
     inside(3)
-    o_wave(2, (2, 3))
     chain(2)
     chain(3)
-    o_wave(3, (0, 1))
+    o_wave(2)
     finish(0)
     finish(1)
     u_relay(0)
-    o_wave(3, (2, 3))
+    o_wave(3)
     finish(2)
     u_relay(1)
     finish(3)

time: 117 us -> 113 us (0.966)
  Pallas kernels: 112 us -> 109 us
    pallas_call x1, Pallas kernels: 112 us -> 109 us  [run_layer(): pl.pallas_call(layer, name='layer', out_shape=(jax.ShapeDtypeStruct((32,...]
where the time goes in v6:
time: 113 us
  Pallas kernels  109 us (96%)
  between operations  3.06 us (3%)
  local copies, waits for them, and re-layouts  1.67 us (1%)
    pallas_call x1, Pallas kernels, run_layer(): pl.pallas_call(layer, name='layer', out_shape=(jax.ShapeDtypeStruct((32,...  109 us

profile of v6, /device:TPU:2, one launch (start us, length us, event | category | flops | bytes accessed | tf_op | source)
XLA Modules:
  0.0 113.3 jit_solution(15242022864095232643)
XLA Ops:
  1.3 108.6 %layer.1 = (bf16[32,4096]{1,0:T(8,128)(2,1)}, f32[1,1]{1,0:T(1,128)}) custom-call(f32[1]{0:T(128)} %bitcast.8.amax_ref, bf16[32,4096]{1,0:T(8,128)(2,1)} %hid_ref.1, bf16[128,1024]{1,0:T(8,128)(2,1)} %wx_ref.1, bf16[128,1,2,128]{3,2,1,0:T(2,128)(2,1)} %wbc_ref.1, bf16[16,128]{1,0:T(8,128)(2,1)} %bitcast.10, f32[4,1024]{1,0:T(4,128)} %conv_x_ref.1, ...), custom_call_target="tpu_custom_call" | custom-call | tf_op jit(solution)/shard_map/layer/pallas_call | solution.py:889
  109.9 1.7 %copy.20 = bf16[32,4096]{1,0:T(8,128)(2,1)} copy(bf16[32,4096]{1,0:T(8,128)(2,1)} %get-tuple-element.8) | data formatting | bytes 524288

commit v7 on v6

--- a/solution.py
+++ b/solution.py
@@ -287,30 +287,16 @@
     for copy in local:
         copy.start()
 
-    maps = wbc_ref[...].astype(f32)
-    wbuf[0][z_rows(0), 0:128] = maps[:, 0, 0, :].astype(bf16)
-    wbuf[0][z_rows(0), 128:256] = maps[:, 0, 1, :].astype(bf16)
-    for_steps = jnp.concatenate([wdt_ref[...].astype(f32), jnp.zeros((112, 128), f32)], axis=0)
-    wbuf[0][z_rows(0), 256:384] = jnp.transpose(for_steps).astype(bf16)
-    par_ref[...] = jnp.zeros((8, 128), f32)
-    par_ref[0:1, 0:16] = bias_ref[...]
-    par_ref[1:2, 0:16] = decay_ref[...]
-    par_ref[2:3, 0:16] = skip_ref[...]
-
     def side_by_side(ref, k):
         pair = ref[k, 0].astype(f32)
         return jnp.concatenate([pair[0:1], pair[1:2]], axis=1)
 
     lane = lax.broadcasted_iota(jnp.int32, (128, 1024), 1)
     head = lax.broadcasted_iota(jnp.int32, (128, 1024), 0)
-    expand[...] = jnp.where((lane >= head * 64) & (lane < head * 64 + 64), 1.0, 0.0).astype(f32)
     row_at = lax.broadcasted_iota(jnp.int32, (128, 128), 0)
     col_at = lax.broadcasted_iota(jnp.int32, (128, 128), 1)
     lower = row_at >= col_at
     ones_lower = jnp.where(lower, 1.0, 0.0).astype(f32)
-    init_t[...] = jnp.transpose(init_ref[pl.ds(pl.multiple_of(x * 256, 256), 256), :])
-    for copy in local:
-        copy.wait()
     pl.semaphore_wait(barrier, len(beside) + len(OTHERS))
 
     def z_copy(j, k, d):
@@ -749,9 +735,23 @@
 
     for r in (1, 3, 2):
         go(hx_copy(r))
+    local[4].wait()
     hy_first(0)
+    maps = wbc_ref[...].astype(f32)
+    wbuf[0][z_rows(0), 0:128] = maps[:, 0, 0, :].astype(bf16)
+    wbuf[0][z_rows(0), 128:256] = maps[:, 0, 1, :].astype(bf16)
+    for_steps = jnp.concatenate([wdt_ref[...].astype(f32), jnp.zeros((112, 128), f32)], axis=0)
+    wbuf[0][z_rows(0), 256:384] = jnp.transpose(for_steps).astype(bf16)
     z_step(0, 0)
+    for copy in local[:4] + local[5:]:
+        copy.wait()
     z_step(1, 0)
+    par_ref[...] = jnp.zeros((8, 128), f32)
+    par_ref[0:1, 0:16] = bias_ref[...]
+    par_ref[1:2, 0:16] = decay_ref[...]
+    par_ref[2:3, 0:16] = skip_ref[...]
+    expand[...] = jnp.where((lane >= head * 64) & (lane < head * 64 + 64), 1.0, 0.0).astype(f32)
+    init_t[...] = jnp.transpose(init_ref[pl.ds(pl.multiple_of(x * 256, 256), 256), :])
     hy_first(1)
     hy_first(3)
     z_step(0, 1)
@@ -763,9 +763,9 @@
     z_step(1, 2)
     z_step(2, 0)
     hy_pass(3)
-    z_step(0, 3)
     z_step(3, 0)
     hy_pass(2)
+    z_step(0, 3)
     z_step(1, 3)
     z_step(2, 1)
     z_step(4, 0)
@@ -825,13 +825,13 @@
     finish(2)
     u_relay(1)
     finish(3)
+    take(weights.at[:, pl.ds(0, 128)], o_last.at[0])
+    multiply(0)
     u_relay(2)
+    y_first(0)
+    u_relay(3)
     for n in range(7):
         go(sq_copy(n))
-    take(weights.at[:, pl.ds(0, 128)], o_last.at[0])
-    multiply(0)
-    y_first(0)
-    u_relay(3)
     take(tokens.at[0, pl.ds(0, 128)], u_last.at[0])
     multiply(3)
     y_add(0)

time: 113 us -> 112 us (level); the launches traced: 113 us -> 111 us
  Pallas kernels: 109 us -> 106 us
    pallas_call x1, Pallas kernels: 109 us -> 106 us  [run_layer(): pl.pallas_call(layer, name='layer', out_shape=(jax.ShapeDtypeStruct((32,...]
where the time goes in v7:
time: 112 us; the launch traced here: 111 us
  Pallas kernels  106 us (95%)
  between operations  3.06 us (3%)
  local copies, waits for them, and re-layouts  1.67 us (1%)
    pallas_call x1, Pallas kernels, run_layer(): pl.pallas_call(layer, name='layer', out_shape=(jax.ShapeDtypeStruct((32,...  106 us

profile of v7, /device:TPU:2, one launch (start us, length us, event | category | flops | bytes accessed | tf_op | source)
XLA Modules:
  0.0 111.0 jit_solution(6768001037655504985)
XLA Ops:
  1.3 106.2 %layer.1 = (bf16[32,4096]{1,0:T(8,128)(2,1)}, f32[1,1]{1,0:T(1,128)}) custom-call(f32[1]{0:T(128)} %bitcast.8.amax_ref, bf16[32,4096]{1,0:T(8,128)(2,1)} %hid_ref.1, bf16[128,1024]{1,0:T(8,128)(2,1)} %wx_ref.1, bf16[128,1,2,128]{3,2,1,0:T(2,128)(2,1)} %wbc_ref.1, bf16[16,128]{1,0:T(8,128)(2,1)} %bitcast.10, f32[4,1024]{1,0:T(4,128)} %conv_x_ref.1, ...), custom_call_target="tpu_custom_call" | custom-call | tf_op jit(solution)/shard_map/layer/pallas_call | solution.py:889
  107.5 1.7 %copy.20 = bf16[32,4096]{1,0:T(8,128)(2,1)} copy(bf16[32,4096]{1,0:T(8,128)(2,1)} %get-tuple-element.8) | data formatting | bytes 524288
